TPU v7x, 32 devices: a whole 2x2x4 slice. The times are simulated.
32 devices in a mesh: lon: 16 (over z, x, core), lat: 2 (over y).
Axes of the slice: x: 2, y: 2, z: 4, core: 2. Of those that a mesh axis runs over, the one named last changes fastest.
Arguments:
- thermal_anomaly_array: float32 [16, 256, 256], P(None, 'lon', 'lat'), may hold values from -6 to 6
- saltiness_anomaly_array: float32 [16, 256, 256], P(None, 'lon', 'lat'), may hold values from -6 to 6
- zonal_volume_passage: float32 [16, 256, 256], P(None, 'lon', 'lat'), may hold values from -0.15 to 0.15
- meridional_volume_passage: float32 [16, 256, 256], P(None, 'lon', 'lat'), may hold values from -0.15 to 0.15
- rising_volume_passage: float32 [15, 256, 256], P(None, 'lon', 'lat'), may hold values from -0.15 to 0.15
- diffusive_coupling_number: float32 [15, 256, 256], P(None, 'lon', 'lat'), may hold values from 0.05 to 2
- sea_column_flag: int32 [256, 256], P('lon', 'lat'), may hold values 0 or 1
- seabed_layer_index: int32 [256, 256], P('lon', 'lat'), may hold values from 1 to 16
Outputs:
- new_temperature: float32 [16, 256, 256], P(None, 'lon', 'lat')
- new_salinity: float32 [16, 256, 256], P(None, 'lon', 'lat')
All inputs are finite; a program needn't handle non-finite values. No bound on the sum of `sea_column_flag` on one device may be relied on, other than what follows from the above.
Results may differ from a plain program's by a relative error of at most 0.0003.
Values sent between devices are 32-bit elements; how exact they have to be, the bound alone decides.
No kernel may reach another device: no remote copies, remote signals or barrier semaphores. Data moves between devices by JAX's collectives and lax.ppermute only.
A program may use at most 64 MiB of HBM per device.

v0:
```python
import jax
import jax.numpy as jnp
from jax import lax
from jax.experimental import pallas as pl
from jax.experimental.pallas import tpu as pltpu
from jax.sharding import PartitionSpec as P


FLUX_FLOOR = 0.01
BIG = 1e30
AXES = ("lon", "lat")
F32 = jnp.float32


SPOTS = (("t", 0, 3), ("s", 3, 3), ("u", 6, 2), ("v", 8, 3), ("w", 11, 2), ("m", 13, 3))
OWN = 12
UNROLL = (4, 4, 4)


def roll(x, shift, axis):
    if not isinstance(shift, int):
        return pltpu.roll(x, shift, axis)
    shift = shift % x.shape[axis]
    return x if shift == 0 else pltpu.roll(x, shift, axis)


def position():
    return lax.axis_index("lon"), lax.axis_index("lat")


def by_parity(body):
    even = lax.rem(lax.axis_index("lon"), 2) == 0

    @pl.when(even)
    def _():
        body(True)

    @pl.when(jnp.logical_not(even))
    def _():
        body(False)


def lanes_of(rows, lanes):
    lane = lax.broadcasted_iota(jnp.int32, (rows, lanes), 1)
    return lane, lane >> 4, lane & 15


def wet_of(flag, depth, level):
    return jnp.where((level < depth) & (flag > 0), 1.0, 0.0).astype(F32)


def pack(
    t_any, s_any, u_any, v_any, w_any, dc_any, flag_any, depth_any,
    core, chip, chip1, diag1, lat1, top, own, t, s, u, v, w, dc, flag, depth, sems,
):
    sources = (flag_any, depth_any, t_any, s_any, u_any, v_any, w_any, dc_any)
    targets = (flag, depth, t, s, u, v, w, dc)
    copies = [pltpu.make_async_copy(x, y, sems.at[n]) for n, (x, y) in enumerate(zip(sources, targets))]
    for copy in copies:
        copy.start()
    levels, rows, lanes = t.shape
    _, j = position()
    _, group, spot = lanes_of(rows, lanes)
    zero = jnp.zeros((rows, lanes), F32)
    core[levels] = zero
    chip1[...] = jnp.zeros(chip1.shape, F32)
    diag1[...] = jnp.zeros(diag1.shape, F32)
    for copy in copies:
        copy.wait()
    flags, depths = flag[...], depth[...]
    fields = dict(t=t, s=s, u=u, v=v, w=w)
    held = {}
    for n, (name, _, _) in enumerate(SPOTS):
        for parity in range(2):
            out = zero
            for g in range(levels // 2):
                k = 2 * g + parity
                if name == "w" and k == levels - 1:
                    continue
                x = wet_of(flags, depths, k) if name == "m" else fields[name][k]
                out = jnp.where(group == g, roll(x, 16 * g + 6, 1), out)
            own[n, parity] = out
            held[name, parity] = out
    tops, afar = [], []
    for parity in range(2):
        up, down = zero, zero
        for name, start, count in SPOTS:
            mine = (spot >= start) & (spot < start + count)
            up = jnp.where(mine, roll(held[name, parity], start - (6 - count), 1), up)
            down = jnp.where(mine, roll(held[name, parity], start - 6, 1), down)
        top[parity] = up
        afar.append(jnp.where(j == 0, up, down))
        lat1[parity] = afar[parity]
        tops.append(up)

    def sides(out, east):
        a, c = (rows - 3, rows - 2) if east else (0, 0)
        for k in range(levels):
            out[k, 0:3] = t[k, a : a + 3]
            out[k, 3:6] = s[k, a : a + 3]
            out[k, 6:9] = u[k, a : a + 3]
            out[k, 9:11] = v[k, c : c + 2]
            if k < levels - 1:
                out[k, 11:13] = w[k, c : c + 2]
            else:
                out[k, 11:13] = jnp.zeros((2, lanes), F32)
            out[k, 13:16] = wet_of(flags, depths, k)[a : a + 3]

    def fill(even):
        sides(core, even)
        sides(chip, not even)
        for out, east, edges in ((core.at[levels], even, tops), (chip1, not even, tops), (diag1, not even, afar)):
            a = rows - 3 if east else 0
            for n, x in enumerate(edges):
                out[3 * n : 3 * n + 3] = x[a : a + 3]

    by_parity(fill)


def repack(top, core, chip1, lat1, core2, fold):
    levels = core.shape[0] - 1
    rows, _ = top.shape[1:]
    wide = rows + 8
    fold[...] = jnp.zeros(fold.shape, F32)
    core2[...] = jnp.zeros(core2.shape, F32)
    for parity in range(2):
        fold[wide * parity + 4 : wide * parity + 4 + rows] = top[parity]

    def fill(even):
        for parity in range(2):
            near, far = core[levels, 3 * parity : 3 * parity + 3], chip1[3 * parity : 3 * parity + 3]
            east, west = (near, far) if even else (far, near)
            at = wide * parity
            fold[at + 1 : at + 4] = west
            fold[at + rows + 4 : at + rows + 7] = east
            a, b = (rows - 3, 0) if even else (0, rows - 3)
            core2[3 * parity : 3 * parity + 3] = lat1[parity, a : a + 3]
            at = 2 * wide + 3 * parity
            fold[at : at + 3] = lat1[parity, b : b + 3]

    by_parity(fill)


def prepare(t, s, u, v, w, dc, flag, depth, number, inverse, ct, cs, cu, cv, cw, cm):
    levels, rows, _ = t.shape
    flags, depths = flag[...], depth[...]
    zero = jnp.zeros(flags.shape, F32)
    q = [zero]
    for k in range(1, levels):
        q.append(dc[k - 1] * wet_of(flags, depths, k))
    q.append(zero)
    ratio = zero
    for k in range(levels):
        denom = 1.0 + q[k] + q[k + 1] - q[k] * ratio
        inv = 1.0 / denom
        ratio = q[k + 1] * inv
        number[k] = q[k]
        inverse[k] = inv
    for ref in (ct, cs, cu, cv, cw, cm):
        for k in (0, levels + 1):
            ref[k] = jnp.zeros(ref.shape[1:], F32)
    for k in range(levels):
        ct[k + 1, OWN : OWN + rows] = t[k]
        cs[k + 1, OWN : OWN + rows] = s[k]
        cu[k + 1, OWN : OWN + rows] = u[k]
        cv[k + 1, OWN : OWN + rows] = v[k]
        cw[k + 1, OWN : OWN + rows] = w[k] if k < levels - 1 else zero
        cm[k + 1, OWN : OWN + rows] = wet_of(flags, depths, k)


def low_and_anti(speed):
    parts = jnp.maximum(speed, 0.0), jnp.minimum(speed, 0.0), 0.5 * jnp.abs(speed)
    return lambda a, b: (parts[0] * a + parts[1] * b, parts[2] * (b - a))


def limited(anti, rise_a, drop_a, rise_b, drop_b):
    return anti * jnp.where(anti >= 0.0, jnp.minimum(rise_b, drop_a), jnp.minimum(rise_a, drop_b))


def ratios(lowered, top_value, low_value, inward, outward):
    gain = sum(jnp.maximum(x, 0.0) for x in inward) - sum(jnp.minimum(x, 0.0) for x in outward)
    loss = gain + (sum(outward) - sum(inward))
    rise = jnp.minimum(1.0, (top_value - lowered) / jnp.maximum(gain, FLUX_FLOOR))
    drop = jnp.minimum(1.0, (lowered - low_value) / jnp.maximum(loss, FLUX_FLOOR))
    return rise, drop


def main(
    ct_in, cs_in, cu_in, cv_in, cw_in, cm_in, core, chip,
    adv_t, adv_s, sides, ct, cs, cu, cv, cw, cm,
    low_t, low_s, ae_t, ae_s, an_t, an_s, au_t, au_s, hi_t, hi_s, lo_t, lo_s, up_t, up_s, dn_t, dn_s, fe_t, fe_s,
):
    levels, rows, lanes = adv_t.shape
    wide = rows + 8
    here, to_east, to_west = pl.ds(8, wide), pl.ds(9, wide), pl.ds(7, wide)
    inner = pl.ds(OWN, rows)

    def fill(even):
        for src, east in ((core, even), (chip, not even)):
            a = OWN + rows if east else OWN - 3
            b = OWN + rows if east else OWN - 2
            for k in range(levels):
                ct[k + 1, a : a + 3] = src[k, 0:3]
                cs[k + 1, a : a + 3] = src[k, 3:6]
                cu[k + 1, a : a + 3] = src[k, 6:9]
                cv[k + 1, b : b + 2] = src[k, 9:11]
                cw[k + 1, b : b + 2] = src[k, 11:13]
                cm[k + 1, a : a + 3] = src[k, 13:16]

    by_parity(fill)

    tracers = (
        (ct, low_t, ae_t, an_t, au_t, hi_t, lo_t, up_t, dn_t, fe_t, adv_t),
        (cs, low_s, ae_s, an_s, au_s, hi_s, lo_s, up_s, dn_s, fe_s, adv_s),
    )
    nothing = jnp.zeros((wide, lanes), F32)
    for _, low, ae, an, au, hi, lo, rise, drop, _, _ in tracers:
        au[0, here] = nothing
        for k in (0, levels + 1):
            hi[k, here] = nothing - BIG
            lo[k, here] = nothing + BIG
            rise[k, here] = nothing
            drop[k, here] = nothing

    def first_pass(k, carry):
        wet = cm[k, here]
        east = low_and_anti(cu[k, here] * (wet * cm[k, to_east]))
        north = low_and_anti(cv[k, here] * (wet * roll(wet, -1, 1)))
        upward = low_and_anti(cw[k, here] * (wet * cm[k + 1, here]))
        fluxes = []
        for n, (c, low, ae, an, au, hi, lo, _, _, face, _) in enumerate(tracers):
            x = c[k, here]
            fe, ae[k, here] = east(x, c[k, to_east])
            fn, an[k, here] = north(x, roll(x, -1, 1))
            fu, au[k, here] = upward(c[k + 1, here], x)
            face[k, here] = fe
            fluxes.append(fu)
            lowered = x - ((fe - face[k, to_west]) + (fn - roll(fn, 1, 1)) + (carry[n] - fu))
            low[k, here] = lowered
            dry = wet == 0.0
            hi[k, here] = jnp.where(dry, -BIG, jnp.maximum(x, lowered))
            lo[k, here] = jnp.where(dry, BIG, jnp.minimum(x, lowered))
        return tuple(fluxes)

    lax.fori_loop(1, levels + 1, first_pass, (nothing, nothing), unroll=UNROLL[0])

    def second_pass(k, carry):
        for _, low, ae, an, au, hi, lo, rise, drop, _, _ in tracers:
            top_value, low_value = hi[k, here], lo[k, here]
            for x in (hi[k, to_east], hi[k, to_west], roll(top_value, -1, 1), roll(top_value, 1, 1),
                      hi[k + 1, here], hi[k - 1, here]):
                top_value = jnp.maximum(top_value, x)
            for x in (lo[k, to_east], lo[k, to_west], roll(low_value, -1, 1), roll(low_value, 1, 1),
                      lo[k + 1, here], lo[k - 1, here]):
                low_value = jnp.minimum(low_value, x)
            anti_n = an[k, here]
            rise[k, here], drop[k, here] = ratios(
                low[k, here], top_value, low_value,
                (ae[k, to_west], roll(anti_n, 1, 1), au[k, here]), (ae[k, here], anti_n, au[k - 1, here]),
            )
        return carry

    lax.fori_loop(1, levels + 1, second_pass, 0, unroll=UNROLL[1])

    def third_pass(k, carry):
        fluxes = []
        for n, (_, low, ae, an, au, _, _, rise, drop, face, adv) in enumerate(tracers):
            r, d = rise[k, here], drop[k, here]
            fe = limited(ae[k, here], r, d, rise[k, to_east], drop[k, to_east])
            face[k, here] = fe
            r, d = rise[k, inner], drop[k, inner]
            fn = limited(an[k, inner], r, d, roll(r, -1, 1), roll(d, -1, 1))
            fu = limited(au[k, inner], rise[k + 1, inner], drop[k + 1, inner], r, d)
            fluxes.append(fu)
            out = (face[k, inner] - face[k, pl.ds(OWN - 1, rows)]) + (fn - roll(fn, 1, 1)) + (carry[n] - fu)
            adv[k - 1] = low[k, inner] - out
        return tuple(fluxes)

    no_flux = jnp.zeros((rows, lanes), F32)
    lax.fori_loop(1, levels + 1, third_pass, (no_flux, no_flux), unroll=UNROLL[2])

    _, group, _ = lanes_of(rows, lanes)
    for n, src in enumerate((core, chip)):
        for parity in range(2):
            out = no_flux
            for g in range(levels // 2):
                out = jnp.where(group == g, roll(src[2 * g + parity], 16 * g + 6, 1), out)
            sides[n, parity] = out


def finish(
    adv_t, adv_s, number, inverse, own, sides, top, lat1, core2, diag1, fold,
    new_t, new_s,
    ct, cs, cu, cv, cw, cm, edge, mirror,
    low_t, low_s, ae_t, ae_s, an_t, an_s, au_t, au_s, hi_t, hi_s, lo_t, lo_s, up_t, up_s, dn_t, dn_s, fe_t, fe_s,
):
    i, j = position()
    n_lon, n_lat = lax.axis_size("lon"), lax.axis_size("lat")
    first, last, is_top, is_low = i == 0, i == n_lon - 1, j == n_lat - 1, j == 0
    levels, rows, lanes = adv_t.shape
    wide = rows + 8
    _, group, spot = lanes_of(wide, lanes)
    here, to_east, to_west = pl.ds(8, wide), pl.ds(9, wide), pl.ds(7, wide)
    cells = (ct, cs, cu, cv, cw, cm)
    starts = (0, 3, 6, 9, 11, 13)
    counts = (3, 3, 3, 2, 2, 3)

    for n, ref in enumerate(cells):
        for parity in range(2):
            ref[2 + parity, OWN : OWN + rows] = own[n, parity]
    for parity in range(2):
        edge[parity, 4 : 4 + rows] = lat1[parity]
        edge[2 + parity] = fold[wide * parity : wide * parity + wide]

    def fill(even):
        for n, (src, east) in enumerate(((core2, even), (diag1, not even))):
            for ref, start, count in zip(cells, starts, counts):
                a = OWN + rows if east else OWN - count
                for parity in range(2):
                    ref[2 + parity, a : a + count] = sides[n, parity, start : start + count]
            a = 4 + rows if east else 1
            for parity in range(2):
                edge[parity, a : a + 3] = src[3 * parity : 3 * parity + 3]

    by_parity(fill)

    @pl.when(first)
    def _():
        for parity in range(2):
            edge[parity, 1:4] = fold[2 * wide + 3 * parity : 2 * wide + 3 * parity + 3]
            edge[2 + parity, rows + 4 : rows + 7] = top[parity, 0:3]

    @pl.when(last)
    def _():
        for parity in range(2):
            edge[parity, rows + 4 : rows + 7] = fold[2 * wide + 3 * parity : 2 * wide + 3 * parity + 3]
            edge[2 + parity, 1:4] = top[parity, rows - 3 : rows]

    for parity in range(2):
        for r in range(wide):
            q = wide - 1 - r
            mirror[parity, r : r + 1] = edge[2 + parity, q : q + 1]

    for parity in range(2):
        other, mir = edge[parity], mirror[parity]
        for ref, (name, start, count) in zip(cells, SPOTS):
            mine = ref[2 + parity, here]
            source = mir
            if name == "u":
                source = -roll(mir, -1, 0)
            if name == "v":
                source = -mir
            beyond = roll(other, 6 - start, 1)
            lead = start + 1 if name == "v" else start + count - 1
            for d in range(2 if name == "v" else count):
                beyond = jnp.where((spot == 6 + d) & is_top, roll(source, 6 + d - (lead - d), 1), beyond)
            value_n = jnp.where(spot < 6, mine, beyond)
            if name == "v":
                folded = 0.5 * (mine + roll(source, 5 - (start + 2), 1))
                value_n = jnp.where((spot == 5) & is_top, folded, value_n)
            value_s = jnp.where(spot < 6, roll(other, 6 - count - start, 1), mine)
            if name == "m":
                value_n = jnp.where(spot > 8, 0.0, value_n)
                value_s = jnp.where((spot < 3) | (spot > 11) | ((spot < 6) & is_low), 0.0, value_s)
            ref[parity, here] = value_n
            ref[2 + parity, here] = value_s

    lowest = group == levels // 2 - 1
    highest = group == 0

    def below(ref, k, edge_value=None):
        if k % 2 == 0:
            return ref[k + 1, here]
        x = roll(ref[k - 1, here], -16, 1)
        return x if edge_value is None else jnp.where(lowest, edge_value, x)

    def above(ref, k, edge_value):
        if k % 2 == 1:
            return ref[k - 1, here]
        return jnp.where(highest, edge_value, roll(ref[k + 1, here], 16, 1))

    tracers = (
        (ct, low_t, ae_t, an_t, au_t, hi_t, lo_t, up_t, dn_t, fe_t),
        (cs, low_s, ae_s, an_s, au_s, hi_s, lo_s, up_s, dn_s, fe_s),
    )
    for strip in (0, 2):
        ends = (strip, strip + 1)
        tops = [[None, None], [None, None]]
        for k in ends:
            wet = cm[k, here]
            east = low_and_anti(cu[k, here] * (wet * cm[k, to_east]))
            north = low_and_anti(cv[k, here] * (wet * roll(wet, -1, 1)))
            upward = low_and_anti(cw[k, here] * (wet * below(cm, k, 0.0)))
            for n, (c, low, ae, an, au, hi, lo, _, _, face) in enumerate(tracers):
                x = c[k, here]
                fe, ae[k, here] = east(x, c[k, to_east])
                fn, an[k, here] = north(x, roll(x, -1, 1))
                fu, au[k, here] = upward(below(c, k), x)
                face[k, here] = fe
                tops[n][k % 2] = fu
                low[k, here] = x - ((fe - face[k, to_west]) + (fn - roll(fn, 1, 1)) - fu)
        for k in ends:
            dry = cm[k, here] == 0.0
            for n, (c, low, ae, an, au, hi, lo, _, _, _) in enumerate(tracers):
                over = tops[n][0] if k % 2 == 1 else jnp.where(highest, 0.0, roll(tops[n][1], 16, 1))
                x, lowered = c[k, here], low[k, here] - over
                low[k, here] = lowered
                hi[k, here] = jnp.where(dry, -BIG, jnp.maximum(x, lowered))
                lo[k, here] = jnp.where(dry, BIG, jnp.minimum(x, lowered))
        for k in ends:
            for _, low, ae, an, au, hi, lo, rise, drop, _ in tracers:
                top_value, low_value = hi[k, here], lo[k, here]
                for x in (hi[k, to_east], hi[k, to_west], roll(top_value, -1, 1), roll(top_value, 1, 1),
                          below(hi, k, -BIG), above(hi, k, -BIG)):
                    top_value = jnp.maximum(top_value, x)
                for x in (lo[k, to_east], lo[k, to_west], roll(low_value, -1, 1), roll(low_value, 1, 1),
                          below(lo, k, BIG), above(lo, k, BIG)):
                    low_value = jnp.minimum(low_value, x)
                anti_n = an[k, here]
                rise[k, here], drop[k, here] = ratios(
                    low[k, here], top_value, low_value,
                    (ae[k, to_west], roll(anti_n, 1, 1), au[k, here]), (ae[k, here], anti_n, above(au, k, 0.0)),
                )
        for k in ends:
            for _, low, ae, an, au, hi, _, rise, drop, face in tracers:
                r, d = rise[k, here], drop[k, here]
                face[k, here] = limited(ae[k, here], r, d, rise[k, to_east], drop[k, to_east])
                hi[k, here] = limited(au[k, here], below(rise, k), below(drop, k), r, d)
        for k in ends:
            for _, low, ae, an, au, hi, lo, rise, drop, face in tracers:
                r, d = rise[k, here], drop[k, here]
                fn = limited(an[k, here], r, d, roll(r, -1, 1), roll(d, -1, 1))
                out = (face[k, here] - face[k, to_west]) + (fn - roll(fn, 1, 1))
                lo[k, here] = low[k, here] - (out + (above(hi, k, 0.0) - hi[k, here]))

    _, _, place = lanes_of(rows, lanes)
    ends = []
    for tracer in tracers:
        lo = tracer[6]
        ends.append([
            jnp.where(place < 6, lo[parity, OWN : OWN + rows], lo[2 + parity, OWN : OWN + rows])
            for parity in range(2)
        ])
    lane, _, _ = lanes_of(rows, lanes)
    outer = (lane < 3) | (lane >= lanes - 3)
    solved = [None, None]
    for k in range(levels):
        q, inv = number[k], inverse[k]
        for n, adv in enumerate((adv_t, adv_s)):
            x = jnp.where(outer, roll(ends[n][k % 2], -(16 * (k // 2) + 6), 1), adv[k])
            if k > 0:
                x = x + q * solved[n]
            solved[n] = x * inv
            (new_t, new_s)[n][k] = solved[n]
    for k in range(levels - 2, -1, -1):
        ratio = number[k + 1] * inverse[k]
        for n, out in enumerate((new_t, new_s)):
            solved[n] = out[k] + ratio * solved[n]
            out[k] = solved[n]


def call(body, outs, args, scratch=(), aliases=None, limit=8, flops=2_000_000):
    vmem = pl.BlockSpec(memory_space=pltpu.VMEM)
    outs = [x if hasattr(x, "dtype") else jax.ShapeDtypeStruct(x, F32) for x in outs]
    where = pltpu.HBM if body is pack else pltpu.VMEM
    return pl.pallas_call(
        body,
        out_shape=tuple(outs),
        in_specs=[pl.BlockSpec(memory_space=where)] * len(args),
        out_specs=tuple(vmem for _ in outs),
        scratch_shapes=[x if not isinstance(x, tuple) else pltpu.VMEM(x, F32) for x in scratch],
        input_output_aliases=aliases or {},
        compiler_params=pltpu.CompilerParams(vmem_limit_bytes=limit * 2**20),
        cost_estimate=pl.CostEstimate(flops=flops, bytes_accessed=2_000_000, transcendentals=0),
    )(*args)


def local(n_lon, n_lat, *args):
    levels, rows, lanes = args[0].shape
    wide = rows + 8

    def number(i, j):
        return (i % n_lon) * n_lat + j

    grid = [(i, j) for i in range(n_lon) for j in range(n_lat)]
    north = n_lat - 1

    def beside(i):
        return i - 1 if i % 2 == 0 else i + 1

    cores = [(number(i, j), number(i ^ 1, j)) for i, j in grid]
    chips = [(number(i, j), number(beside(i), j)) for i, j in grid]
    inner = [(number(i, j), number(beside(i), j)) for i, j in grid if 0 <= beside(i) < n_lon]
    diags = [(number(i, j), number(beside(i), n_lat - 1 - j)) for i, j in grid if 0 <= beside(i) < n_lon]
    lats = [(number(i, j), number(i, n_lat - 1 - j)) for i, j in grid]
    folds = [(number(i, j), number(n_lon - 1 - i, j)) for i, j in grid if j == north or i in (0, n_lon - 1)]

    def send(x, pairs):
        return lax.ppermute(x, AXES, pairs)

    core, chip, chip1, diag1, lat1, top, own, *held = call(
        pack,
        [(levels + 1, rows, lanes), (levels, rows, lanes), (8, lanes), (8, lanes), (2, rows, lanes), (2, rows, lanes),
         (6, 2, rows, lanes)] + [jax.ShapeDtypeStruct(x.shape, x.dtype) for x in args],
        [pltpu.with_memory_space_constraint(x, pltpu.HBM) for x in args],
        [pltpu.SemaphoreType.DMA((len(args),))],
    )
    chip1_in = send(chip1, inner)
    lat1_in = send(lat1, lats)
    core_in = send(core, cores)
    diag1_in = send(diag1, diags)
    chip_in = send(chip, chips)
    cell = (levels + 2, 40, lanes)
    numbers, inverse, *cells = call(prepare, [(levels, rows, lanes)] * 2 + [cell] * 6, held)
    core2, fold = call(repack, [(8, lanes), (2 * wide + 8, lanes)], (top, core_in, chip1_in, lat1_in), limit=2)
    fold_in = send(fold, folds)
    core2_in = send(core2, cores)
    adv_t, adv_s, sides, *_ = call(
        main,
        [(levels, rows, lanes)] * 2 + [(2, 2, rows, lanes)] + [cell] * 6,
        (*cells, core_in, chip_in),
        [cell] * 18,
        aliases={n: 3 + n for n in range(6)},
        limit=20,
        flops=20_000_000,
    )
    strip = (4, 40, lanes)
    return call(
        finish,
        [(levels, rows, lanes)] * 2,
        (adv_t, adv_s, numbers, inverse, own, sides, top, lat1_in, core2_in, diag1_in, fold_in),
        [strip] * 6 + [(4, wide, lanes), (2, wide, lanes)] + [strip] * 18,
    )


def solution(mesh):
    n_lon, n_lat = mesh.shape["lon"], mesh.shape["lat"]
    cube = P(None, "lon", "lat")
    plane = P("lon", "lat")
    return jax.shard_map(
        lambda *args: tuple(local(n_lon, n_lat, *args)),
        mesh=mesh,
        in_specs=(cube,) * 6 + (plane,) * 2,
        out_specs=(cube, cube),
        check_vma=False,
    )
```

profile of v0, /device:TPU:9, one launch (start us, length us, event | category | flops | bytes accessed | tf_op | source)
XLA Modules:
  0.0 25.3 jit_solution(16665770116866831907)
XLA Ops:
  0.6 1.7 %shard_map.95 = (f32[17,16,128]{2,1,0:T(8,128)S(1)}, f32[16,16,128]{2,1,0:T(8,128)S(1)}, f32[8,128]{1,0:T(8,128)S(1)}, f32[8,128]{1,0:T(8,128)S(1)}, f32[2,16,12...) custom-call(f32[16,16,128]{2,1,0:T(8,128)} %t_any.1, ...), custom_call_target="tpu_custom_call" | custom-call | flops 2000000 | bytes 2000000 | tf_op jit(solution)/shard_map/pallas_call | solution.py:466
  2.3 0.7 %collective-permute-start = (f32[17,16,128]{2,1,0:T(8,128)S(1)}, f32[17,16,128]{2,1,0:T(8,128)S(1)}, u32[]{:S(2)}, u32[]{:S(2)}) collective-permute-start(f32[17,16,128]{2,1,0:T(8,128)S(1)} %get-tuple-element.44), channel_id=1, source_target_pairs={{0,2},{1,3},{2,0},{3,1},{4,6},{5,7},{6,4},{7,5},{8,10},{9,11},{10,... | collective-permute-start | bytes 417800 | tf_op jit(solution)/shard_map/ppermute | solution.py:499
  3.0 1.2 %collective-permute-start.1 = (f32[16,16,128]{2,1,0:T(8,128)S(1)}, f32[16,16,128]{2,1,0:T(8,128)S(1)}, u32[]{:S(2)}, u32[]{:S(2)}) collective-permute-start(f32[16,16,128]{2,1,0:T(8,128)S(1)} %get-tuple-element.45), channel_id=1, source_target_pairs={{0,30},{1,31},{2,4},{3,5},{4,2},{5,3},{6,8},{7,9},{8,6},{9,7},{10,... | collective-permute-start | bytes 393224 | tf_op jit(solution)/shard_map/ppermute | solution.py:499
  4.2 1.2 %collective-permute-start.2 = (f32[2,16,128]{2,1,0:T(8,128)S(1)}, f32[2,16,128]{2,1,0:T(8,128)S(1)}, u32[]{:S(2)}, u32[]{:S(2)}) collective-permute-start(f32[2,16,128]{2,1,0:T(8,128)S(1)} %get-tuple-element.53), channel_id=1, source_target_pairs={{0,1},{1,0},{2,3},{3,2},{4,5},{5,4},{6,7},{7,6},{8,9},{9,8},{10,11... | collective-permute-start | bytes 49160 | tf_op jit(solution)/shard_map/ppermute | solution.py:499
  5.5 2.7 %collective-permute-start.3 = (f32[8,128]{1,0:T(8,128)S(1)}, f32[8,128]{1,0:T(8,128)S(1)}, u32[]{:S(2)}, u32[]{:S(2)}) collective-permute-start(f32[8,128]{1,0:T(8,128)S(1)} %get-tuple-element.54), channel_id=1, source_target_pairs={{2,4},{3,5},{4,2},{5,3},{6,8},{7,9},{8,6},{9,7},{10,12},{11,13},{1... | collective-permute-start | bytes 12296 | tf_op jit(solution)/shard_map/ppermute | solution.py:499
  8.2 2.2 %collective-permute-done.3.chip1 = f32[8,128]{1,0:T(8,128)S(1)} collective-permute-done((f32[8,128]{1,0:T(8,128)S(1)}, f32[8,128]{1,0:T(8,128)S(1)}, u32[]{:S(2)}, u32[]{:S(2)}) %collective-permute-start.3) | collective-permute-done | bytes 4128 | tf_op jit(solution)/shard_map/ppermute | solution.py:499
  10.4 0.0 collective-permute-done.2.lat1
  10.4 0.0 collective-permute-done.core
  10.4 0.7 %collective-permute-start.6 = (f32[56,128]{1,0:T(8,128)S(1)}, f32[56,128]{1,0:T(8,128)S(1)}, u32[]{:S(2)}, u32[]{:S(2)}) collective-permute-start(f32[56,128]{1,0:T(8,128)S(1)} %get-tuple-element.57), channel_id=1, source_target_pairs={{0,30},{1,31},{3,29},{5,27},{7,25},{9,23},{11,21},{13,19},{15,17},... | collective-permute-start | bytes 86024 | tf_op jit(solution)/shard_map/ppermute | solution.py:499
  11.1 5.9 %collective-permute-start.5 = (f32[8,128]{1,0:T(8,128)S(1)}, f32[8,128]{1,0:T(8,128)S(1)}, u32[]{:S(2)}, u32[]{:S(2)}) collective-permute-start(f32[8,128]{1,0:T(8,128)S(1)} %get-tuple-element.56), channel_id=1, source_target_pairs={{2,5},{3,4},{4,3},{5,2},{6,9},{7,8},{8,7},{9,6},{10,13},{11,12},{1... | collective-permute-start | bytes 12296 | tf_op jit(solution)/shard_map/ppermute | solution.py:499
  16.9 3.5 %collective-permute-start.4 = (f32[8,128]{1,0:T(8,128)S(1)}, f32[8,128]{1,0:T(8,128)S(1)}, u32[]{:S(2)}, u32[]{:S(2)}) collective-permute-start(f32[8,128]{1,0:T(8,128)S(1)} %get-tuple-element.55), channel_id=1, source_target_pairs={{0,2},{1,3},{2,0},{3,1},{4,6},{5,7},{6,4},{7,5},{8,10},{9,11},{10,... | collective-permute-start | bytes 12296 | tf_op jit(solution)/shard_map/ppermute | solution.py:499
  20.4 0.1 shard_map.96
  20.6 0.0 collective-permute-done.1.chip
  20.6 2.7 %shard_map.97 = (f32[16,16,128]{2,1,0:T(8,128)S(1)}, f32[16,16,128]{2,1,0:T(8,128)S(1)}, f32[2,2,16,128]{3,2,1,0:T(8,128)S(1)}, f32[18,40,128]{2,1,0:T(8,128)S(1...) custom-call(f32[18,40,128]{2,1,0:T(8,128)S(1)} %get-tuple-element.38, ...), custom_call_target="tpu_custom_call", output_to_operand_aliasing={{3}: (0, {}), {4}: (1, {}), {5}: (2, {}), {6}: (3, {}), {7}... | custom-call | flops 20000000 | bytes 2000000 | tf_op jit(solution)/shard_map/pallas_call | solution.py:466
  23.3 0.0 collective-permute-done.5.diag1
  23.3 0.0 collective-permute-done.4.core2
  23.3 0.0 collective-permute-done.6.fold
  23.3 1.9 %shard_map.99 = (f32[16,16,128]{2,1,0:T(8,128)}, f32[16,16,128]{2,1,0:T(8,128)}) custom-call(f32[16,16,128]{2,1,0:T(8,128)S(1)} %get-tuple-element.46.adv_t, f32[16,16,128]{2,1,0:T(8,128)S(1)} %get-tuple-element.47.adv_s, f32[16,16,128]{2,1,0:T(8,128)S(1)} %get-tuple-element.48.number, f32[16,16,128]{2,1,0:T(8,128)S(1)} %get-tuple-element.49.inverse, ...), custom_call_target="tpu_custom_call" | custom-call | flops 2000000 | bytes 2000000 | tf_op jit(solution)/shard_map/pallas_call | solution.py:466
  (1 shorter events, 0.0 us)
Async XLA Ops:
  2.3 8.0 %collective-permute-start = (f32[17,16,128]{2,1,0:T(8,128)S(1)}, f32[17,16,128]{2,1,0:T(8,128)S(1)}, u32[]{:S(2)}, u32[]{:S(2)}) collective-permute-start(f32[17,16,128]{2,1,0:T(8,128)S(1)} %get-tuple-element.44), channel_id=1, source_target_pairs={{0,2},{1,3},{2,0},{3,1},{4,6},{5,7},{6,4},{7,5},{8,10},{9,11},{10,... | collective-permute-start | bytes 417800 | tf_op jit(solution)/shard_map/ppermute | solution.py:499
  3.0 17.5 %collective-permute-start.1 = (f32[16,16,128]{2,1,0:T(8,128)S(1)}, f32[16,16,128]{2,1,0:T(8,128)S(1)}, u32[]{:S(2)}, u32[]{:S(2)}) collective-permute-start(f32[16,16,128]{2,1,0:T(8,128)S(1)} %get-tuple-element.45), channel_id=1, source_target_pairs={{0,30},{1,31},{2,4},{3,5},{4,2},{5,3},{6,8},{7,9},{8,6},{9,7},{10,... | collective-permute-start | bytes 393224 | tf_op jit(solution)/shard_map/ppermute | solution.py:499
  4.2 6.2 %collective-permute-start.2 = (f32[2,16,128]{2,1,0:T(8,128)S(1)}, f32[2,16,128]{2,1,0:T(8,128)S(1)}, u32[]{:S(2)}, u32[]{:S(2)}) collective-permute-start(f32[2,16,128]{2,1,0:T(8,128)S(1)} %get-tuple-element.53), channel_id=1, source_target_pairs={{0,1},{1,0},{2,3},{3,2},{4,5},{5,4},{6,7},{7,6},{8,9},{9,8},{10,11... | collective-permute-start | bytes 49160 | tf_op jit(solution)/shard_map/ppermute | solution.py:499
  5.5 4.9 %collective-permute-start.3 = (f32[8,128]{1,0:T(8,128)S(1)}, f32[8,128]{1,0:T(8,128)S(1)}, u32[]{:S(2)}, u32[]{:S(2)}) collective-permute-start(f32[8,128]{1,0:T(8,128)S(1)} %get-tuple-element.54), channel_id=1, source_target_pairs={{2,4},{3,5},{4,2},{5,3},{6,8},{7,9},{8,6},{9,7},{10,12},{11,13},{1... | collective-permute-start | bytes 12296 | tf_op jit(solution)/shard_map/ppermute | solution.py:499
  10.4 12.9 %collective-permute-start.6 = (f32[56,128]{1,0:T(8,128)S(1)}, f32[56,128]{1,0:T(8,128)S(1)}, u32[]{:S(2)}, u32[]{:S(2)}) collective-permute-start(f32[56,128]{1,0:T(8,128)S(1)} %get-tuple-element.57), channel_id=1, source_target_pairs={{0,30},{1,31},{3,29},{5,27},{7,25},{9,23},{11,21},{13,19},{15,17},... | collective-permute-start | bytes 86024 | tf_op jit(solution)/shard_map/ppermute | solution.py:499
  11.1 12.2 %collective-permute-start.5 = (f32[8,128]{1,0:T(8,128)S(1)}, f32[8,128]{1,0:T(8,128)S(1)}, u32[]{:S(2)}, u32[]{:S(2)}) collective-permute-start(f32[8,128]{1,0:T(8,128)S(1)} %get-tuple-element.56), channel_id=1, source_target_pairs={{2,5},{3,4},{4,3},{5,2},{6,9},{7,8},{8,7},{9,6},{10,13},{11,12},{1... | collective-permute-start | bytes 12296 | tf_op jit(solution)/shard_map/ppermute | solution.py:499
  16.9 6.3 %collective-permute-start.4 = (f32[8,128]{1,0:T(8,128)S(1)}, f32[8,128]{1,0:T(8,128)S(1)}, u32[]{:S(2)}, u32[]{:S(2)}) collective-permute-start(f32[8,128]{1,0:T(8,128)S(1)} %get-tuple-element.55), channel_id=1, source_target_pairs={{0,2},{1,3},{2,0},{3,1},{4,6},{5,7},{6,4},{7,5},{8,10},{9,11},{10,... | collective-permute-start | bytes 12296 | tf_op jit(solution)/shard_map/ppermute | solution.py:499
where the time goes:
time: 25.5 us; the launch traced here: 25.3 us
  starting transfers between devices  15.9 us (62%)
  Pallas kernels  6.49 us (25%)
  waiting for transfers between devices  2.17 us (9%)
  between operations  0.72 us (3%)
    ppermute x7, starting transfers between devices, send(): return lax.ppermute(x, AXES, pairs)  15.9 us
    pallas_call x5, Pallas kernels, call(): pl.pallas_call(body, out_shape=tuple(outs), in_specs=[pl.BlockSpec(memory...  6.49 us
    ppermute x7, waiting for transfers between devices, send(): return lax.ppermute(x, AXES, pairs)  2.17 us
  transfers between devices with their start and end apart: 7, of which 1 were waited for; matrix products, arithmetic and copies ran while one was open for 0% of the time, Pallas kernels for 11%

commit v1 on v0

--- a/solution.py
+++ b/solution.py
@@ -483,17 +483,17 @@
         return (i % n_lon) * n_lat + j
 
     grid = [(i, j) for i in range(n_lon) for j in range(n_lat)]
-    north = n_lat - 1
 
     def beside(i):
         return i - 1 if i % 2 == 0 else i + 1
 
     cores = [(number(i, j), number(i ^ 1, j)) for i, j in grid]
     chips = [(number(i, j), number(beside(i), j)) for i, j in grid]
-    inner = [(number(i, j), number(beside(i), j)) for i, j in grid if 0 <= beside(i) < n_lon]
-    diags = [(number(i, j), number(beside(i), n_lat - 1 - j)) for i, j in grid if 0 <= beside(i) < n_lon]
     lats = [(number(i, j), number(i, n_lat - 1 - j)) for i, j in grid]
-    folds = [(number(i, j), number(n_lon - 1 - i, j)) for i, j in grid if j == north or i in (0, n_lon - 1)]
+    folds = [(number(i, j), number(n_lon - 1 - i, j)) for i, j in grid]
+    ends = [(number(i, j), number(i, n_lat - 1 - j)) for i, j in grid if i in (0, n_lon - 1)]
+    inner = [(number(i, j), number(beside(i), j)) for i, j in grid if 0 < i < n_lon - 1] + ends
+    diags = [(number(i, j), number(beside(i), n_lat - 1 - j)) for i, j in grid if 0 < i < n_lon - 1] + ends
 
     def send(x, pairs):
         return lax.ppermute(x, AXES, pairs)

time: 25.5 us -> 21.9 us (0.86)
  the two profiles are of different devices: /device:TPU:9 before, /device:TPU:0 now
where the time goes in v1:
time: 21.9 us; the launch traced here: 21.6 us
  starting transfers between devices  10.6 us (48%)
  Pallas kernels  6.46 us (29%)
  waiting for transfers between devices  3.86 us (18%)
  between operations  0.7 us (3%)
    ppermute x7, starting transfers between devices, send(): return lax.ppermute(x, AXES, pairs)  10.6 us
    pallas_call x5, Pallas kernels, call(): pl.pallas_call(body, out_shape=tuple(outs), in_specs=[pl.BlockSpec(memory...  6.46 us
    ppermute x7, waiting for transfers between devices, send(): return lax.ppermute(x, AXES, pairs)  3.86 us
  transfers between devices with their start and end apart: 7, of which 2 were waited for; matrix products, arithmetic and copies ran while one was open for 0% of the time, Pallas kernels for 13%

profile of v1, /device:TPU:0, one launch (start us, length us, event | category | flops | bytes accessed | tf_op | source)
XLA Modules:
  0.0 21.6 jit_solution(3133071016756351677)
XLA Ops:
  0.6 1.7 %shard_map.95 = (f32[17,16,128]{2,1,0:T(8,128)S(1)}, f32[16,16,128]{2,1,0:T(8,128)S(1)}, f32[8,128]{1,0:T(8,128)S(1)}, f32[8,128]{1,0:T(8,128)S(1)}, f32[2,16,12...) custom-call(f32[16,16,128]{2,1,0:T(8,128)} %t_any.1, ...), custom_call_target="tpu_custom_call" | custom-call | flops 2000000 | bytes 2000000 | tf_op jit(solution)/shard_map/pallas_call | solution.py:466
  2.3 0.6 %collective-permute-start = (f32[17,16,128]{2,1,0:T(8,128)S(1)}, f32[17,16,128]{2,1,0:T(8,128)S(1)}, u32[]{:S(2)}, u32[]{:S(2)}) collective-permute-start(f32[17,16,128]{2,1,0:T(8,128)S(1)} %get-tuple-element.44), channel_id=1, source_target_pairs={{0,2},{1,3},{2,0},{3,1},{4,6},{5,7},{6,4},{7,5},{8,10},{9,11},{10,... | collective-permute-start | bytes 417800 | tf_op jit(solution)/shard_map/ppermute | solution.py:499
  2.9 5.6 %collective-permute-start.1 = (f32[16,16,128]{2,1,0:T(8,128)S(1)}, f32[16,16,128]{2,1,0:T(8,128)S(1)}, u32[]{:S(2)}, u32[]{:S(2)}) collective-permute-start(f32[16,16,128]{2,1,0:T(8,128)S(1)} %get-tuple-element.45), channel_id=1, source_target_pairs={{0,30},{1,31},{2,4},{3,5},{4,2},{5,3},{6,8},{7,9},{8,6},{9,7},{10,... | collective-permute-start | bytes 393224 | tf_op jit(solution)/shard_map/ppermute | solution.py:499
  8.5 1.5 %collective-permute-start.2 = (f32[2,16,128]{2,1,0:T(8,128)S(1)}, f32[2,16,128]{2,1,0:T(8,128)S(1)}, u32[]{:S(2)}, u32[]{:S(2)}) collective-permute-start(f32[2,16,128]{2,1,0:T(8,128)S(1)} %get-tuple-element.53), channel_id=1, source_target_pairs={{0,1},{1,0},{2,3},{3,2},{4,5},{5,4},{6,7},{7,6},{8,9},{9,8},{10,11... | collective-permute-start | bytes 49160 | tf_op jit(solution)/shard_map/ppermute | solution.py:499
  10.0 0.5 %collective-permute-start.3 = (f32[8,128]{1,0:T(8,128)S(1)}, f32[8,128]{1,0:T(8,128)S(1)}, u32[]{:S(2)}, u32[]{:S(2)}) collective-permute-start(f32[8,128]{1,0:T(8,128)S(1)} %get-tuple-element.54), channel_id=1, source_target_pairs={{2,4},{3,5},{4,2},{5,3},{6,8},{7,9},{8,6},{9,7},{10,12},{11,13},{1... | collective-permute-start | bytes 12296 | tf_op jit(solution)/shard_map/ppermute | solution.py:499
  10.5 3.1 %collective-permute-done.3.chip1 = f32[8,128]{1,0:T(8,128)S(1)} collective-permute-done((f32[8,128]{1,0:T(8,128)S(1)}, f32[8,128]{1,0:T(8,128)S(1)}, u32[]{:S(2)}, u32[]{:S(2)}) %collective-permute-start.3) | collective-permute-done | bytes 4128 | tf_op jit(solution)/shard_map/ppermute | solution.py:499
  13.6 0.0 collective-permute-done.2.lat1
  13.6 0.0 collective-permute-done.core
  13.7 0.1 collective-permute-start.6
  13.7 0.6 %collective-permute-start.5 = (f32[8,128]{1,0:T(8,128)S(1)}, f32[8,128]{1,0:T(8,128)S(1)}, u32[]{:S(2)}, u32[]{:S(2)}) collective-permute-start(f32[8,128]{1,0:T(8,128)S(1)} %get-tuple-element.56), channel_id=1, source_target_pairs={{2,5},{3,4},{4,3},{5,2},{6,9},{7,8},{8,7},{9,6},{10,13},{11,12},{1... | collective-permute-start | bytes 12296 | tf_op jit(solution)/shard_map/ppermute | solution.py:499
  14.3 1.8 %collective-permute-start.4 = (f32[8,128]{1,0:T(8,128)S(1)}, f32[8,128]{1,0:T(8,128)S(1)}, u32[]{:S(2)}, u32[]{:S(2)}) collective-permute-start(f32[8,128]{1,0:T(8,128)S(1)} %get-tuple-element.55), channel_id=1, source_target_pairs={{0,2},{1,3},{2,0},{3,1},{4,6},{5,7},{6,4},{7,5},{8,10},{9,11},{10,... | collective-permute-start | bytes 12296 | tf_op jit(solution)/shard_map/ppermute | solution.py:499
  16.1 0.1 shard_map.96
  16.2 0.0 collective-permute-done.1.chip
  16.2 2.7 %shard_map.97 = (f32[16,16,128]{2,1,0:T(8,128)S(1)}, f32[16,16,128]{2,1,0:T(8,128)S(1)}, f32[2,2,16,128]{3,2,1,0:T(8,128)S(1)}, f32[18,40,128]{2,1,0:T(8,128)S(1...) custom-call(f32[18,40,128]{2,1,0:T(8,128)S(1)} %get-tuple-element.38, ...), custom_call_target="tpu_custom_call", output_to_operand_aliasing={{3}: (0, {}), {4}: (1, {}), {5}: (2, {}), {6}: (3, {}), {7}... | custom-call | flops 20000000 | bytes 2000000 | tf_op jit(solution)/shard_map/pallas_call | solution.py:466
  18.9 0.0 collective-permute-done.5.diag1
  19.0 0.0 collective-permute-done.4.core2
  19.0 0.7 %collective-permute-done.6.fold = f32[56,128]{1,0:T(8,128)S(1)} collective-permute-done((f32[56,128]{1,0:T(8,128)S(1)}, f32[56,128]{1,0:T(8,128)S(1)}, u32[]{:S(2)}, u32[]{:S(2)}) %collective-permute-start.6) | collective-permute-done | bytes 28704 | tf_op jit(solution)/shard_map/ppermute | solution.py:499
  19.7 1.9 %shard_map.99 = (f32[16,16,128]{2,1,0:T(8,128)}, f32[16,16,128]{2,1,0:T(8,128)}) custom-call(f32[16,16,128]{2,1,0:T(8,128)S(1)} %get-tuple-element.46.adv_t, f32[16,16,128]{2,1,0:T(8,128)S(1)} %get-tuple-element.47.adv_s, f32[16,16,128]{2,1,0:T(8,128)S(1)} %get-tuple-element.48.number, f32[16,16,128]{2,1,0:T(8,128)S(1)} %get-tuple-element.49.inverse, ...), custom_call_target="tpu_custom_call" | custom-call | flops 2000000 | bytes 2000000 | tf_op jit(solution)/shard_map/pallas_call | solution.py:466
  (1 shorter events, 0.0 us)
Async XLA Ops:
  2.3 11.3 %collective-permute-start = (f32[17,16,128]{2,1,0:T(8,128)S(1)}, f32[17,16,128]{2,1,0:T(8,128)S(1)}, u32[]{:S(2)}, u32[]{:S(2)}) collective-permute-start(f32[17,16,128]{2,1,0:T(8,128)S(1)} %get-tuple-element.44), channel_id=1, source_target_pairs={{0,2},{1,3},{2,0},{3,1},{4,6},{5,7},{6,4},{7,5},{8,10},{9,11},{10,... | collective-permute-start | bytes 417800 | tf_op jit(solution)/shard_map/ppermute | solution.py:499
  2.9 13.3 %collective-permute-start.1 = (f32[16,16,128]{2,1,0:T(8,128)S(1)}, f32[16,16,128]{2,1,0:T(8,128)S(1)}, u32[]{:S(2)}, u32[]{:S(2)}) collective-permute-start(f32[16,16,128]{2,1,0:T(8,128)S(1)} %get-tuple-element.45), channel_id=1, source_target_pairs={{0,30},{1,31},{2,4},{3,5},{4,2},{5,3},{6,8},{7,9},{8,6},{9,7},{10,... | collective-permute-start | bytes 393224 | tf_op jit(solution)/shard_map/ppermute | solution.py:499
  8.5 5.1 %collective-permute-start.2 = (f32[2,16,128]{2,1,0:T(8,128)S(1)}, f32[2,16,128]{2,1,0:T(8,128)S(1)}, u32[]{:S(2)}, u32[]{:S(2)}) collective-permute-start(f32[2,16,128]{2,1,0:T(8,128)S(1)} %get-tuple-element.53), channel_id=1, source_target_pairs={{0,1},{1,0},{2,3},{3,2},{4,5},{5,4},{6,7},{7,6},{8,9},{9,8},{10,11... | collective-permute-start | bytes 49160 | tf_op jit(solution)/shard_map/ppermute | solution.py:499
  10.0 3.6 %collective-permute-start.3 = (f32[8,128]{1,0:T(8,128)S(1)}, f32[8,128]{1,0:T(8,128)S(1)}, u32[]{:S(2)}, u32[]{:S(2)}) collective-permute-start(f32[8,128]{1,0:T(8,128)S(1)} %get-tuple-element.54), channel_id=1, source_target_pairs={{2,4},{3,5},{4,2},{5,3},{6,8},{7,9},{8,6},{9,7},{10,12},{11,13},{1... | collective-permute-start | bytes 12296 | tf_op jit(solution)/shard_map/ppermute | solution.py:499
  13.7 6.1 %collective-permute-start.6 = (f32[56,128]{1,0:T(8,128)S(1)}, f32[56,128]{1,0:T(8,128)S(1)}, u32[]{:S(2)}, u32[]{:S(2)}) collective-permute-start(f32[56,128]{1,0:T(8,128)S(1)} %get-tuple-element.57), channel_id=1, source_target_pairs={{0,30},{1,31},{2,28},{3,29},{4,26},{5,27},{6,24},{7,25},{8,22},{9,... | collective-permute-start | bytes 86024 | tf_op jit(solution)/shard_map/ppermute | solution.py:499
  13.7 5.2 %collective-permute-start.5 = (f32[8,128]{1,0:T(8,128)S(1)}, f32[8,128]{1,0:T(8,128)S(1)}, u32[]{:S(2)}, u32[]{:S(2)}) collective-permute-start(f32[8,128]{1,0:T(8,128)S(1)} %get-tuple-element.56), channel_id=1, source_target_pairs={{2,5},{3,4},{4,3},{5,2},{6,9},{7,8},{8,7},{9,6},{10,13},{11,12},{1... | collective-permute-start | bytes 12296 | tf_op jit(solution)/shard_map/ppermute | solution.py:499
  14.3 4.7 %collective-permute-start.4 = (f32[8,128]{1,0:T(8,128)S(1)}, f32[8,128]{1,0:T(8,128)S(1)}, u32[]{:S(2)}, u32[]{:S(2)}) collective-permute-start(f32[8,128]{1,0:T(8,128)S(1)} %get-tuple-element.55), channel_id=1, source_target_pairs={{0,2},{1,3},{2,0},{3,1},{4,6},{5,7},{6,4},{7,5},{8,10},{9,11},{10,... | collective-permute-start | bytes 12296 | tf_op jit(solution)/shard_map/ppermute | solution.py:499

commit v2 on v1

--- a/solution.py
+++ b/solution.py
@@ -51,7 +51,7 @@
 
 def pack(
     t_any, s_any, u_any, v_any, w_any, dc_any, flag_any, depth_any,
-    core, chip, chip1, diag1, lat1, top, own, t, s, u, v, w, dc, flag, depth, sems,
+    core, chip, chip1, bound, top, own, t, s, u, v, w, dc, flag, depth, sems,
 ):
     sources = (flag_any, depth_any, t_any, s_any, u_any, v_any, w_any, dc_any)
     targets = (flag, depth, t, s, u, v, w, dc)
@@ -64,7 +64,6 @@
     zero = jnp.zeros((rows, lanes), F32)
     core[levels] = zero
     chip1[...] = jnp.zeros(chip1.shape, F32)
-    diag1[...] = jnp.zeros(diag1.shape, F32)
     for copy in copies:
         copy.wait()
     flags, depths = flag[...], depth[...]
@@ -90,7 +89,7 @@
             down = jnp.where(mine, roll(held[name, parity], start - 6, 1), down)
         top[parity] = up
         afar.append(jnp.where(j == 0, up, down))
-        lat1[parity] = afar[parity]
+        bound[parity] = afar[parity]
         tops.append(up)
 
     def sides(out, east):
@@ -109,40 +108,62 @@
     def fill(even):
         sides(core, even)
         sides(chip, not even)
-        for out, east, edges in ((core.at[levels], even, tops), (chip1, not even, tops), (diag1, not even, afar)):
+        for out, east in ((core.at[levels], even), (chip1, not even)):
             a = rows - 3 if east else 0
-            for n, x in enumerate(edges):
+            for n, x in enumerate(tops + afar):
                 out[3 * n : 3 * n + 3] = x[a : a + 3]
 
     by_parity(fill)
 
 
-def repack(top, core, chip1, lat1, core2, fold):
+def repack(top, bound, core, chip1, fold, lat):
     levels = core.shape[0] - 1
     rows, _ = top.shape[1:]
     wide = rows + 8
     fold[...] = jnp.zeros(fold.shape, F32)
-    core2[...] = jnp.zeros(core2.shape, F32)
+    lat[...] = jnp.zeros(lat.shape, F32)
     for parity in range(2):
         fold[wide * parity + 4 : wide * parity + 4 + rows] = top[parity]
+        lat[wide * parity + 4 : wide * parity + 4 + rows] = bound[parity]
+    fold[2 * wide : 2 * wide + 6] = chip1[6:12]
 
     def fill(even):
-        for parity in range(2):
-            near, far = core[levels, 3 * parity : 3 * parity + 3], chip1[3 * parity : 3 * parity + 3]
-            east, west = (near, far) if even else (far, near)
-            at = wide * parity
-            fold[at + 1 : at + 4] = west
-            fold[at + rows + 4 : at + rows + 7] = east
-            a, b = (rows - 3, 0) if even else (0, rows - 3)
-            core2[3 * parity : 3 * parity + 3] = lat1[parity, a : a + 3]
-            at = 2 * wide + 3 * parity
-            fold[at : at + 3] = lat1[parity, b : b + 3]
+        for n, out in enumerate((fold, lat)):
+            for parity in range(2):
+                part = 6 * n + 3 * parity
+                near, far = core[levels, part : part + 3], chip1[part : part + 3]
+                east, west = (near, far) if even else (far, near)
+                at = wide * parity
+                out[at + 1 : at + 4] = west
+                out[at + rows + 4 : at + rows + 7] = east
 
     by_parity(fill)
 
 
-def prepare(t, s, u, v, w, dc, flag, depth, number, inverse, ct, cs, cu, cv, cw, cm):
-    levels, rows, _ = t.shape
+def columns(src, east, cells, levels, rows):
+    ct, cs, cu, cv, cw, cm = cells
+    a = OWN + rows if east else OWN - 3
+    b = OWN + rows if east else OWN - 2
+    for k in range(levels):
+        ct[k + 1, a : a + 3] = src[k, 0:3]
+        cs[k + 1, a : a + 3] = src[k, 3:6]
+        cu[k + 1, a : a + 3] = src[k, 6:9]
+        cv[k + 1, b : b + 2] = src[k, 9:11]
+        cw[k + 1, b : b + 2] = src[k, 11:13]
+        cm[k + 1, a : a + 3] = src[k, 13:16]
+
+
+def at_strips(src, out, levels, rows, lanes):
+    _, group, _ = lanes_of(rows, lanes)
+    for parity in range(2):
+        x = jnp.zeros((rows, lanes), F32)
+        for g in range(levels // 2):
+            x = jnp.where(group == g, roll(src[2 * g + parity], 16 * g + 6, 1), x)
+        out[parity] = x
+
+
+def prepare(t, s, u, v, w, dc, flag, depth, core, number, inverse, core_side, ct, cs, cu, cv, cw, cm):
+    levels, rows, lanes = t.shape
     flags, depths = flag[...], depth[...]
     zero = jnp.zeros(flags.shape, F32)
     q = [zero]
@@ -166,6 +187,8 @@
         cv[k + 1, OWN : OWN + rows] = v[k]
         cw[k + 1, OWN : OWN + rows] = w[k] if k < levels - 1 else zero
         cm[k + 1, OWN : OWN + rows] = wet_of(flags, depths, k)
+    at_strips(core, core_side, levels, rows, lanes)
+    by_parity(lambda even: columns(core, even, (ct, cs, cu, cv, cw, cm), levels, rows))
 
 
 def low_and_anti(speed):
@@ -186,8 +209,8 @@
 
 
 def main(
-    ct_in, cs_in, cu_in, cv_in, cw_in, cm_in, core, chip,
-    adv_t, adv_s, sides, ct, cs, cu, cv, cw, cm,
+    ct_in, cs_in, cu_in, cv_in, cw_in, cm_in, chip,
+    adv_t, adv_s, chip_side, ct, cs, cu, cv, cw, cm,
     low_t, low_s, ae_t, ae_s, an_t, an_s, au_t, au_s, hi_t, hi_s, lo_t, lo_s, up_t, up_s, dn_t, dn_s, fe_t, fe_s,
 ):
     levels, rows, lanes = adv_t.shape
@@ -195,19 +218,7 @@
     here, to_east, to_west = pl.ds(8, wide), pl.ds(9, wide), pl.ds(7, wide)
     inner = pl.ds(OWN, rows)
 
-    def fill(even):
-        for src, east in ((core, even), (chip, not even)):
-            a = OWN + rows if east else OWN - 3
-            b = OWN + rows if east else OWN - 2
-            for k in range(levels):
-                ct[k + 1, a : a + 3] = src[k, 0:3]
-                cs[k + 1, a : a + 3] = src[k, 3:6]
-                cu[k + 1, a : a + 3] = src[k, 6:9]
-                cv[k + 1, b : b + 2] = src[k, 9:11]
-                cw[k + 1, b : b + 2] = src[k, 11:13]
-                cm[k + 1, a : a + 3] = src[k, 13:16]
-
-    by_parity(fill)
+    by_parity(lambda even: columns(chip, not even, (ct, cs, cu, cv, cw, cm), levels, rows))
 
     tracers = (
         (ct, low_t, ae_t, an_t, au_t, hi_t, lo_t, up_t, dn_t, fe_t, adv_t),
@@ -279,17 +290,11 @@
     no_flux = jnp.zeros((rows, lanes), F32)
     lax.fori_loop(1, levels + 1, third_pass, (no_flux, no_flux), unroll=UNROLL[2])
 
-    _, group, _ = lanes_of(rows, lanes)
-    for n, src in enumerate((core, chip)):
-        for parity in range(2):
-            out = no_flux
-            for g in range(levels // 2):
-                out = jnp.where(group == g, roll(src[2 * g + parity], 16 * g + 6, 1), out)
-            sides[n, parity] = out
+    at_strips(chip, chip_side, levels, rows, lanes)
 
 
 def finish(
-    adv_t, adv_s, number, inverse, own, sides, top, lat1, core2, diag1, fold,
+    adv_t, adv_s, number, inverse, own, core_side, chip_side, top, lat, fold,
     new_t, new_s,
     ct, cs, cu, cv, cw, cm, edge, mirror,
     low_t, low_s, ae_t, ae_s, an_t, an_s, au_t, au_s, hi_t, hi_s, lo_t, lo_s, up_t, up_s, dn_t, dn_s, fe_t, fe_s,
@@ -309,18 +314,15 @@
         for parity in range(2):
             ref[2 + parity, OWN : OWN + rows] = own[n, parity]
     for parity in range(2):
-        edge[parity, 4 : 4 + rows] = lat1[parity]
+        edge[parity] = lat[wide * parity : wide * parity + wide]
         edge[2 + parity] = fold[wide * parity : wide * parity + wide]
 
     def fill(even):
-        for n, (src, east) in enumerate(((core2, even), (diag1, not even))):
+        for side, east in ((core_side, even), (chip_side, not even)):
             for ref, start, count in zip(cells, starts, counts):
                 a = OWN + rows if east else OWN - count
                 for parity in range(2):
-                    ref[2 + parity, a : a + count] = sides[n, parity, start : start + count]
-            a = 4 + rows if east else 1
-            for parity in range(2):
-                edge[parity, a : a + 3] = src[3 * parity : 3 * parity + 3]
+                    ref[2 + parity, a : a + count] = side[parity, start : start + count]
 
     by_parity(fill)
 
@@ -493,32 +495,31 @@
     folds = [(number(i, j), number(n_lon - 1 - i, j)) for i, j in grid]
     ends = [(number(i, j), number(i, n_lat - 1 - j)) for i, j in grid if i in (0, n_lon - 1)]
     inner = [(number(i, j), number(beside(i), j)) for i, j in grid if 0 < i < n_lon - 1] + ends
-    diags = [(number(i, j), number(beside(i), n_lat - 1 - j)) for i, j in grid if 0 < i < n_lon - 1] + ends
 
     def send(x, pairs):
         return lax.ppermute(x, AXES, pairs)
 
-    core, chip, chip1, diag1, lat1, top, own, *held = call(
+    core, chip, chip1, bound, top, own, *held = call(
         pack,
-        [(levels + 1, rows, lanes), (levels, rows, lanes), (8, lanes), (8, lanes), (2, rows, lanes), (2, rows, lanes),
-         (6, 2, rows, lanes)] + [jax.ShapeDtypeStruct(x.shape, x.dtype) for x in args],
+        [(levels + 1, rows, lanes), (levels, rows, lanes), (16, lanes)] + [(2, rows, lanes)] * 2
+        + [(6, 2, rows, lanes)] + [jax.ShapeDtypeStruct(x.shape, x.dtype) for x in args],
         [pltpu.with_memory_space_constraint(x, pltpu.HBM) for x in args],
         [pltpu.SemaphoreType.DMA((len(args),))],
     )
     chip1_in = send(chip1, inner)
-    lat1_in = send(lat1, lats)
     core_in = send(core, cores)
-    diag1_in = send(diag1, diags)
     chip_in = send(chip, chips)
     cell = (levels + 2, 40, lanes)
-    numbers, inverse, *cells = call(prepare, [(levels, rows, lanes)] * 2 + [cell] * 6, held)
-    core2, fold = call(repack, [(8, lanes), (2 * wide + 8, lanes)], (top, core_in, chip1_in, lat1_in), limit=2)
+    numbers, inverse, core_side, *cells = call(
+        prepare, [(levels, rows, lanes)] * 2 + [(2, rows, lanes)] + [cell] * 6, (*held, core_in)
+    )
+    fold, lat = call(repack, [(2 * wide + 8, lanes), (2 * wide, lanes)], (top, bound, core_in, chip1_in), limit=2)
     fold_in = send(fold, folds)
-    core2_in = send(core2, cores)
-    adv_t, adv_s, sides, *_ = call(
+    lat_in = send(lat, lats)
+    adv_t, adv_s, chip_side, *_ = call(
         main,
-        [(levels, rows, lanes)] * 2 + [(2, 2, rows, lanes)] + [cell] * 6,
-        (*cells, core_in, chip_in),
+        [(levels, rows, lanes)] * 2 + [(2, rows, lanes)] + [cell] * 6,
+        (*cells, chip_in),
         [cell] * 18,
         aliases={n: 3 + n for n in range(6)},
         limit=20,
@@ -528,7 +529,7 @@
     return call(
         finish,
         [(levels, rows, lanes)] * 2,
-        (adv_t, adv_s, numbers, inverse, own, sides, top, lat1_in, core2_in, diag1_in, fold_in),
+        (adv_t, adv_s, numbers, inverse, own, core_side, chip_side, top, lat_in, fold_in),
         [strip] * 6 + [(4, wide, lanes), (2, wide, lanes)] + [strip] * 18,
     )
 

time: 21.9 us -> 20.4 us (0.932)
  starting transfers between devices: 10.6 us -> 9.36 us
    ppermute x7 -> x5, starting transfers between devices: 10.6 us -> 9.36 us  [send(): return lax.ppermute(x, AXES, pairs)]
    ppermute x7 -> x5, waiting for transfers between devices: 3.86 us -> 3.7 us  [send(): return lax.ppermute(x, AXES, pairs)]
  transfers between devices with their start and end apart: 7 -> 5, of which waited for: 2 -> 2; matrix products, arithmetic and copies ran while one was open for 0% -> 0% of each run, Pallas kernels for 13% -> 14%
where the time goes in v2:
time: 20.4 us; the launch traced here: 20.2 us
  starting transfers between devices  9.36 us (46%)
  Pallas kernels  6.41 us (31%)
  waiting for transfers between devices  3.7 us (18%)
  between operations  0.69 us (3%)
    ppermute x5, starting transfers between devices, send(): return lax.ppermute(x, AXES, pairs)  9.36 us
    pallas_call x5, Pallas kernels, call(): pl.pallas_call(body, out_shape=tuple(outs), in_specs=[pl.BlockSpec(memory...  6.41 us
    ppermute x5, waiting for transfers between devices, send(): return lax.ppermute(x, AXES, pairs)  3.7 us
  transfers between devices with their start and end apart: 5, of which 2 were waited for; matrix products, arithmetic and copies ran while one was open for 0% of the time, Pallas kernels for 14%

profile of v2, /device:TPU:0, one launch (start us, length us, event | category | flops | bytes accessed | tf_op | source)
XLA Modules:
  0.0 20.2 jit_solution(10181490303774180578)
XLA Ops:
  0.6 1.7 %shard_map.95 = (f32[17,16,128]{2,1,0:T(8,128)S(1)}, f32[16,16,128]{2,1,0:T(8,128)S(1)}, f32[16,128]{1,0:T(8,128)S(1)}, f32[2,16,128]{2,1,0:T(8,128)S(1)}, f32[2...) custom-call(f32[16,16,128]{2,1,0:T(8,128)} %t_any.1, ...), custom_call_target="tpu_custom_call" | custom-call | flops 2000000 | bytes 2000000 | tf_op jit(solution)/shard_map/pallas_call | solution.py:468
  2.3 0.6 %collective-permute-start = (f32[17,16,128]{2,1,0:T(8,128)S(1)}, f32[17,16,128]{2,1,0:T(8,128)S(1)}, u32[]{:S(2)}, u32[]{:S(2)}) collective-permute-start(f32[17,16,128]{2,1,0:T(8,128)S(1)} %get-tuple-element.38), channel_id=1, source_target_pairs={{0,2},{1,3},{2,0},{3,1},{4,6},{5,7},{6,4},{7,5},{8,10},{9,11},{10,... | collective-permute-start | bytes 417800 | tf_op jit(solution)/shard_map/ppermute | solution.py:500
  2.9 5.6 %collective-permute-start.1 = (f32[16,16,128]{2,1,0:T(8,128)S(1)}, f32[16,16,128]{2,1,0:T(8,128)S(1)}, u32[]{:S(2)}, u32[]{:S(2)}) collective-permute-start(f32[16,16,128]{2,1,0:T(8,128)S(1)} %get-tuple-element.45), channel_id=1, source_target_pairs={{0,30},{1,31},{2,4},{3,5},{4,2},{5,3},{6,8},{7,9},{8,6},{9,7},{10,... | collective-permute-start | bytes 393224 | tf_op jit(solution)/shard_map/ppermute | solution.py:500
  8.5 1.5 %collective-permute-start.2 = (f32[16,128]{1,0:T(8,128)S(1)}, f32[16,128]{1,0:T(8,128)S(1)}, u32[]{:S(2)}, u32[]{:S(2)}) collective-permute-start(f32[16,128]{1,0:T(8,128)S(1)} %get-tuple-element.55), channel_id=1, source_target_pairs={{2,4},{3,5},{4,2},{5,3},{6,8},{7,9},{8,6},{9,7},{10,12},{11,13},{1... | collective-permute-start | bytes 24584 | tf_op jit(solution)/shard_map/ppermute | solution.py:500
  10.0 2.1 %collective-permute-done.2.chip1 = f32[16,128]{1,0:T(8,128)S(1)} collective-permute-done((f32[16,128]{1,0:T(8,128)S(1)}, f32[16,128]{1,0:T(8,128)S(1)}, u32[]{:S(2)}, u32[]{:S(2)}) %collective-permute-start.2) | collective-permute-done | bytes 8224 | tf_op jit(solution)/shard_map/ppermute | solution.py:500
  12.1 0.0 collective-permute-done.core
  12.2 0.1 collective-permute-start.4
  12.3 1.6 %collective-permute-start.3 = (f32[48,128]{1,0:T(8,128)S(1)}, f32[48,128]{1,0:T(8,128)S(1)}, u32[]{:S(2)}, u32[]{:S(2)}) collective-permute-start(f32[48,128]{1,0:T(8,128)S(1)} %get-tuple-element.56), channel_id=1, source_target_pairs={{0,1},{1,0},{2,3},{3,2},{4,5},{5,4},{6,7},{7,6},{8,9},{9,8},{10,11... | collective-permute-start | bytes 73736 | tf_op jit(solution)/shard_map/ppermute | solution.py:500
  13.8 0.2 shard_map.96
  14.0 0.0 collective-permute-done.1.chip
  14.0 2.6 %shard_map.97 = (f32[16,16,128]{2,1,0:T(8,128)S(1)}, f32[16,16,128]{2,1,0:T(8,128)S(1)}, f32[2,16,128]{2,1,0:T(8,128)S(1)}, f32[18,40,128]{2,1,0:T(8,128)S(1)}, ...) custom-call(f32[18,40,128]{2,1,0:T(8,128)S(1)} %get-tuple-element.39, ...), custom_call_target="tpu_custom_call", output_to_operand_aliasing={{3}: (0, {}), {4}: (1, {}), {5}: (2, {}), {6}: (3, {}), {7}... | custom-call | flops 20000000 | bytes 2000000 | tf_op jit(solution)/shard_map/pallas_call | solution.py:468
  16.7 0.0 collective-permute-done.3.lat
  16.7 1.6 %collective-permute-done.4.fold = f32[56,128]{1,0:T(8,128)S(1)} collective-permute-done((f32[56,128]{1,0:T(8,128)S(1)}, f32[56,128]{1,0:T(8,128)S(1)}, u32[]{:S(2)}, u32[]{:S(2)}) %collective-permute-start.4) | collective-permute-done | bytes 28704 | tf_op jit(solution)/shard_map/ppermute | solution.py:500
  18.2 1.9 %shard_map.99 = (f32[16,16,128]{2,1,0:T(8,128)}, f32[16,16,128]{2,1,0:T(8,128)}) custom-call(f32[16,16,128]{2,1,0:T(8,128)S(1)} %get-tuple-element.46.adv_t, f32[16,16,128]{2,1,0:T(8,128)S(1)} %get-tuple-element.47.adv_s, f32[16,16,128]{2,1,0:T(8,128)S(1)} %get-tuple-element.48.number, f32[16,16,128]{2,1,0:T(8,128)S(1)} %get-tuple-element.49.inverse, ...), custom_call_target="tpu_custom_call" | custom-call | flops 2000000 | bytes 2000000 | tf_op jit(solution)/shard_map/pallas_call | solution.py:468
  (1 shorter events, 0.0 us)
Async XLA Ops:
  2.3 9.8 %collective-permute-start = (f32[17,16,128]{2,1,0:T(8,128)S(1)}, f32[17,16,128]{2,1,0:T(8,128)S(1)}, u32[]{:S(2)}, u32[]{:S(2)}) collective-permute-start(f32[17,16,128]{2,1,0:T(8,128)S(1)} %get-tuple-element.38), channel_id=1, source_target_pairs={{0,2},{1,3},{2,0},{3,1},{4,6},{5,7},{6,4},{7,5},{8,10},{9,11},{10,... | collective-permute-start | bytes 417800 | tf_op jit(solution)/shard_map/ppermute | solution.py:500
  2.9 11.1 %collective-permute-start.1 = (f32[16,16,128]{2,1,0:T(8,128)S(1)}, f32[16,16,128]{2,1,0:T(8,128)S(1)}, u32[]{:S(2)}, u32[]{:S(2)}) collective-permute-start(f32[16,16,128]{2,1,0:T(8,128)S(1)} %get-tuple-element.45), channel_id=1, source_target_pairs={{0,30},{1,31},{2,4},{3,5},{4,2},{5,3},{6,8},{7,9},{8,6},{9,7},{10,... | collective-permute-start | bytes 393224 | tf_op jit(solution)/shard_map/ppermute | solution.py:500
  8.5 3.7 %collective-permute-start.2 = (f32[16,128]{1,0:T(8,128)S(1)}, f32[16,128]{1,0:T(8,128)S(1)}, u32[]{:S(2)}, u32[]{:S(2)}) collective-permute-start(f32[16,128]{1,0:T(8,128)S(1)} %get-tuple-element.55), channel_id=1, source_target_pairs={{2,4},{3,5},{4,2},{5,3},{6,8},{7,9},{8,6},{9,7},{10,12},{11,13},{1... | collective-permute-start | bytes 24584 | tf_op jit(solution)/shard_map/ppermute | solution.py:500
  12.2 6.1 %collective-permute-start.4 = (f32[56,128]{1,0:T(8,128)S(1)}, f32[56,128]{1,0:T(8,128)S(1)}, u32[]{:S(2)}, u32[]{:S(2)}) collective-permute-start(f32[56,128]{1,0:T(8,128)S(1)} %get-tuple-element.57), channel_id=1, source_target_pairs={{0,30},{1,31},{2,28},{3,29},{4,26},{5,27},{6,24},{7,25},{8,22},{9,... | collective-permute-start | bytes 86024 | tf_op jit(solution)/shard_map/ppermute | solution.py:500
  12.3 4.4 %collective-permute-start.3 = (f32[48,128]{1,0:T(8,128)S(1)}, f32[48,128]{1,0:T(8,128)S(1)}, u32[]{:S(2)}, u32[]{:S(2)}) collective-permute-start(f32[48,128]{1,0:T(8,128)S(1)} %get-tuple-element.56), channel_id=1, source_target_pairs={{0,1},{1,0},{2,3},{3,2},{4,5},{5,4},{6,7},{7,6},{8,9},{9,8},{10,11... | collective-permute-start | bytes 73736 | tf_op jit(solution)/shard_map/ppermute | solution.py:500

commit v3 on v2

--- a/solution.py
+++ b/solution.py
@@ -14,7 +14,7 @@
 
 SPOTS = (("t", 0, 3), ("s", 3, 3), ("u", 6, 2), ("v", 8, 3), ("w", 11, 2), ("m", 13, 3))
 OWN = 12
-UNROLL = (4, 4, 4)
+UNROLL = (8, 8, 8)
 
 
 def roll(x, shift, axis):
@@ -51,7 +51,7 @@
 
 def pack(
     t_any, s_any, u_any, v_any, w_any, dc_any, flag_any, depth_any,
-    core, chip, chip1, bound, top, own, t, s, u, v, w, dc, flag, depth, sems,
+    chip1, bound, top, own, t, s, u, v, w, dc, flag, depth, sems,
 ):
     sources = (flag_any, depth_any, t_any, s_any, u_any, v_any, w_any, dc_any)
     targets = (flag, depth, t, s, u, v, w, dc)
@@ -62,14 +62,15 @@
     _, j = position()
     _, group, spot = lanes_of(rows, lanes)
     zero = jnp.zeros((rows, lanes), F32)
-    core[levels] = zero
     chip1[...] = jnp.zeros(chip1.shape, F32)
-    for copy in copies:
+    for copy in copies[:2]:
         copy.wait()
     flags, depths = flag[...], depth[...]
     fields = dict(t=t, s=s, u=u, v=v, w=w)
     held = {}
-    for n, (name, _, _) in enumerate(SPOTS):
+    for n, name in ((5, "m"), (0, "t"), (1, "s"), (2, "u"), (3, "v"), (4, "w")):
+        if name != "m":
+            copies[2 + n].wait()
         for parity in range(2):
             out = zero
             for g in range(levels // 2):
@@ -80,17 +81,36 @@
                 out = jnp.where(group == g, roll(x, 16 * g + 6, 1), out)
             own[n, parity] = out
             held[name, parity] = out
-    tops, afar = [], []
-    for parity in range(2):
-        up, down = zero, zero
+    edges = []
+    for parity in range(2):
+        up, down, across = zero, zero, zero
         for name, start, count in SPOTS:
+            x = held[name, parity]
             mine = (spot >= start) & (spot < start + count)
-            up = jnp.where(mine, roll(held[name, parity], start - (6 - count), 1), up)
-            down = jnp.where(mine, roll(held[name, parity], start - 6, 1), down)
-        top[parity] = up
-        afar.append(jnp.where(j == 0, up, down))
-        bound[parity] = afar[parity]
-        tops.append(up)
+            up = jnp.where(mine, roll(x, start - (6 - count), 1), up)
+            down = jnp.where(mine, roll(x, start - 6, 1), down)
+            x = -x if name in ("u", "v") else x
+            for d in range(count):
+                at = (4, 3, 5)[d] if name == "v" else 5 - d
+                across = jnp.where(spot == start + d, roll(x, start + d - at, 1), across)
+        top[parity] = across
+        bound[parity] = jnp.where(j == 0, up, down)
+        edges.append(across)
+    edges += [bound[0], bound[1]]
+
+    def fill(even):
+        a = 0 if even else rows - 3
+        for n, x in enumerate(edges):
+            chip1[3 * n : 3 * n + 3] = x[a : a + 3]
+
+    by_parity(fill)
+    copies[7].wait()
+
+
+def pack_columns(t, s, u, v, w, flag, depth, bound, top, core, chip):
+    levels, rows, lanes = t.shape
+    flags, depths = flag[...], depth[...]
+    core[levels] = jnp.zeros((rows, lanes), F32)
 
     def sides(out, east):
         a, c = (rows - 3, rows - 2) if east else (0, 0)
@@ -108,10 +128,11 @@
     def fill(even):
         sides(core, even)
         sides(chip, not even)
-        for out, east in ((core.at[levels], even), (chip1, not even)):
-            a = rows - 3 if east else 0
-            for n, x in enumerate(tops + afar):
-                out[3 * n : 3 * n + 3] = x[a : a + 3]
+        a = rows - 3 if even else 0
+        for n, x in enumerate((top, bound)):
+            for parity in range(2):
+                at = 6 * n + 3 * parity
+                core[levels, at : at + 3] = x[parity, a : a + 3]
 
     by_parity(fill)
 
@@ -162,7 +183,7 @@
         out[parity] = x
 
 
-def prepare(t, s, u, v, w, dc, flag, depth, core, number, inverse, core_side, ct, cs, cu, cv, cw, cm):
+def prepare(t, s, u, v, w, dc, flag, depth, core, inverse, onward, back, core_side, ct, cs, cu, cv, cw, cm):
     levels, rows, lanes = t.shape
     flags, depths = flag[...], depth[...]
     zero = jnp.zeros(flags.shape, F32)
@@ -175,8 +196,9 @@
         denom = 1.0 + q[k] + q[k + 1] - q[k] * ratio
         inv = 1.0 / denom
         ratio = q[k + 1] * inv
-        number[k] = q[k]
         inverse[k] = inv
+        onward[k] = q[k] * inv
+        back[k] = ratio
     for ref in (ct, cs, cu, cv, cw, cm):
         for k in (0, levels + 1):
             ref[k] = jnp.zeros(ref.shape[1:], F32)
@@ -293,38 +315,138 @@
     at_strips(chip, chip_side, levels, rows, lanes)
 
 
+def strip_advection(scratch, levels, rows, lanes):
+    (ct, cs, cu, cv, cw, cm, low_t, low_s, ae_t, ae_s, an_t, an_s, au_t, au_s, hi_t, hi_s, lo_t, lo_s,
+     up_t, up_s, dn_t, dn_s, fe_t, fe_s) = scratch
+    wide = rows + 8
+    _, group, _ = lanes_of(wide, lanes)
+    here, to_east, to_west = pl.ds(8, wide), pl.ds(9, wide), pl.ds(7, wide)
+    lowest = group == levels // 2 - 1
+    highest = group == 0
+
+    def below(ref, k, edge_value=None):
+        if k % 2 == 0:
+            return ref[k + 1, here]
+        x = roll(ref[k - 1, here], -16, 1)
+        return x if edge_value is None else jnp.where(lowest, edge_value, x)
+
+    def above(ref, k, edge_value):
+        if k % 2 == 1:
+            return ref[k - 1, here]
+        return jnp.where(highest, edge_value, roll(ref[k + 1, here], 16, 1))
+
+    tracers = (
+        (ct, low_t, ae_t, an_t, au_t, hi_t, lo_t, up_t, dn_t, fe_t),
+        (cs, low_s, ae_s, an_s, au_s, hi_s, lo_s, up_s, dn_s, fe_s),
+    )
+    ends = (0, 1)
+    tops = [[None, None], [None, None]]
+    for k in ends:
+        wet = cm[k, here]
+        east = low_and_anti(cu[k, here] * (wet * cm[k, to_east]))
+        north = low_and_anti(cv[k, here] * (wet * roll(wet, -1, 1)))
+        upward = low_and_anti(cw[k, here] * (wet * below(cm, k, 0.0)))
+        for n, (c, low, ae, an, au, hi, lo, _, _, face) in enumerate(tracers):
+            x = c[k, here]
+            fe, ae[k, here] = east(x, c[k, to_east])
+            fn, an[k, here] = north(x, roll(x, -1, 1))
+            fu, au[k, here] = upward(below(c, k), x)
+            face[k, here] = fe
+            tops[n][k % 2] = fu
+            low[k, here] = x - ((fe - face[k, to_west]) + (fn - roll(fn, 1, 1)) - fu)
+    for k in ends:
+        dry = cm[k, here] == 0.0
+        for n, (c, low, ae, an, au, hi, lo, _, _, _) in enumerate(tracers):
+            over = tops[n][0] if k % 2 == 1 else jnp.where(highest, 0.0, roll(tops[n][1], 16, 1))
+            x, lowered = c[k, here], low[k, here] - over
+            low[k, here] = lowered
+            hi[k, here] = jnp.where(dry, -BIG, jnp.maximum(x, lowered))
+            lo[k, here] = jnp.where(dry, BIG, jnp.minimum(x, lowered))
+    for k in ends:
+        for _, low, ae, an, au, hi, lo, rise, drop, _ in tracers:
+            top_value, low_value = hi[k, here], lo[k, here]
+            for x in (hi[k, to_east], hi[k, to_west], roll(top_value, -1, 1), roll(top_value, 1, 1),
+                      below(hi, k, -BIG), above(hi, k, -BIG)):
+                top_value = jnp.maximum(top_value, x)
+            for x in (lo[k, to_east], lo[k, to_west], roll(low_value, -1, 1), roll(low_value, 1, 1),
+                      below(lo, k, BIG), above(lo, k, BIG)):
+                low_value = jnp.minimum(low_value, x)
+            anti_n = an[k, here]
+            rise[k, here], drop[k, here] = ratios(
+                low[k, here], top_value, low_value,
+                (ae[k, to_west], roll(anti_n, 1, 1), au[k, here]), (ae[k, here], anti_n, above(au, k, 0.0)),
+            )
+    for k in ends:
+        for _, low, ae, an, au, hi, _, rise, drop, face in tracers:
+            r, d = rise[k, here], drop[k, here]
+            face[k, here] = limited(ae[k, here], r, d, rise[k, to_east], drop[k, to_east])
+            hi[k, here] = limited(au[k, here], below(rise, k), below(drop, k), r, d)
+    for k in ends:
+        for _, low, ae, an, au, hi, lo, rise, drop, face in tracers:
+            r, d = rise[k, here], drop[k, here]
+            fn = limited(an[k, here], r, d, roll(r, -1, 1), roll(d, -1, 1))
+            out = (face[k, here] - face[k, to_west]) + (fn - roll(fn, 1, 1))
+            lo[k, here] = low[k, here] - (out + (above(hi, k, 0.0) - hi[k, here]))
+
+
+def strip_cells(scratch, own, core_side, chip_side):
+    cells, rows = scratch[:6], own.shape[2]
+    for n, ref in enumerate(cells):
+        for parity in range(2):
+            ref[parity, OWN : OWN + rows] = own[n, parity]
+
+    def fill(even):
+        for side, east in ((core_side, even), (chip_side, not even)):
+            for ref, start, count in zip(cells, (0, 3, 6, 9, 11, 13), (3, 3, 3, 2, 2, 3)):
+                a = OWN + rows if east else OWN - count
+                for parity in range(2):
+                    ref[parity, a : a + count] = side[parity, start : start + count]
+
+    by_parity(fill)
+
+
+def south_strip(scratch, own, core_side, chip_side, edge, levels, out):
+    rows, lanes = own.shape[2:]
+    wide = rows + 8
+    _, _, spot = lanes_of(wide, lanes)
+    _, j = position()
+    here = pl.ds(8, wide)
+    strip_cells(scratch, own, core_side, chip_side)
+    for parity in range(2):
+        for ref, (name, start, count) in zip(scratch, SPOTS):
+            value = jnp.where(spot < 6, roll(edge[parity], 6 - count - start, 1), ref[parity, here])
+            if name == "m":
+                value = jnp.where((spot < 3) | (spot > 11) | ((spot < 6) & (j == 0)), 0.0, value)
+            ref[parity, here] = value
+    strip_advection(scratch, levels, rows, lanes)
+    for n in range(2):
+        for parity in range(2):
+            out[n, parity] = scratch[16 + n][parity, OWN : OWN + rows]
+
+
+def south(adv_t, own, core_side, chip_side, lat, out, edge, *scratch):
+    levels, rows, _ = adv_t.shape
+    for parity in range(2):
+        edge[parity] = lat[(rows + 8) * parity : (rows + 8) * (parity + 1)]
+    south_strip(scratch, own, core_side, chip_side, edge, levels, out)
+
+
 def finish(
-    adv_t, adv_s, number, inverse, own, core_side, chip_side, top, lat, fold,
-    new_t, new_s,
-    ct, cs, cu, cv, cw, cm, edge, mirror,
-    low_t, low_s, ae_t, ae_s, an_t, an_s, au_t, au_s, hi_t, hi_s, lo_t, lo_s, up_t, up_s, dn_t, dn_s, fe_t, fe_s,
+    adv_t, adv_s, inverse, onward, back, own, core_side, chip_side, top, lat, fold, south_in,
+    new_t, new_s, edge, mirror, south_end, *scratch,
 ):
     i, j = position()
     n_lon, n_lat = lax.axis_size("lon"), lax.axis_size("lat")
-    first, last, is_top, is_low = i == 0, i == n_lon - 1, j == n_lat - 1, j == 0
+    first, last, is_top = i == 0, i == n_lon - 1, j == n_lat - 1
     levels, rows, lanes = adv_t.shape
     wide = rows + 8
-    _, group, spot = lanes_of(wide, lanes)
-    here, to_east, to_west = pl.ds(8, wide), pl.ds(9, wide), pl.ds(7, wide)
-    cells = (ct, cs, cu, cv, cw, cm)
-    starts = (0, 3, 6, 9, 11, 13)
-    counts = (3, 3, 3, 2, 2, 3)
-
-    for n, ref in enumerate(cells):
-        for parity in range(2):
-            ref[2 + parity, OWN : OWN + rows] = own[n, parity]
+    _, _, spot = lanes_of(wide, lanes)
+    here = pl.ds(8, wide)
+
     for parity in range(2):
         edge[parity] = lat[wide * parity : wide * parity + wide]
         edge[2 + parity] = fold[wide * parity : wide * parity + wide]
-
-    def fill(even):
-        for side, east in ((core_side, even), (chip_side, not even)):
-            for ref, start, count in zip(cells, starts, counts):
-                a = OWN + rows if east else OWN - count
-                for parity in range(2):
-                    ref[2 + parity, a : a + count] = side[parity, start : start + count]
-
-    by_parity(fill)
+    south_end[...] = south_in[...]
 
     @pl.when(first)
     def _():
@@ -338,126 +460,48 @@
             edge[parity, rows + 4 : rows + 7] = fold[2 * wide + 3 * parity : 2 * wide + 3 * parity + 3]
             edge[2 + parity, 1:4] = top[parity, rows - 3 : rows]
 
+    @pl.when((first | last) & (j > 0))
+    def _():
+        south_strip(scratch, own, core_side, chip_side, edge, levels, south_end)
+
     for parity in range(2):
         for r in range(wide):
             q = wide - 1 - r
             mirror[parity, r : r + 1] = edge[2 + parity, q : q + 1]
 
+    strip_cells(scratch, own, core_side, chip_side)
+    _, u_start, u_count = SPOTS[2]
     for parity in range(2):
         other, mir = edge[parity], mirror[parity]
-        for ref, (name, start, count) in zip(cells, SPOTS):
-            mine = ref[2 + parity, here]
-            source = mir
-            if name == "u":
-                source = -roll(mir, -1, 0)
-            if name == "v":
-                source = -mir
-            beyond = roll(other, 6 - start, 1)
-            lead = start + 1 if name == "v" else start + count - 1
-            for d in range(2 if name == "v" else count):
-                beyond = jnp.where((spot == 6 + d) & is_top, roll(source, 6 + d - (lead - d), 1), beyond)
-            value_n = jnp.where(spot < 6, mine, beyond)
+        mir = jnp.where((spot >= u_start) & (spot < u_start + u_count), roll(mir, -1, 0), mir)
+        source = jnp.where(is_top, mir, other)
+        for ref, (name, start, count) in zip(scratch, SPOTS):
+            mine = ref[parity, here]
+            value = jnp.where(spot < 6, mine, roll(source, 6 - start, 1))
             if name == "v":
                 folded = 0.5 * (mine + roll(source, 5 - (start + 2), 1))
-                value_n = jnp.where((spot == 5) & is_top, folded, value_n)
-            value_s = jnp.where(spot < 6, roll(other, 6 - count - start, 1), mine)
+                value = jnp.where((spot == 5) & is_top, folded, value)
             if name == "m":
-                value_n = jnp.where(spot > 8, 0.0, value_n)
-                value_s = jnp.where((spot < 3) | (spot > 11) | ((spot < 6) & is_low), 0.0, value_s)
-            ref[parity, here] = value_n
-            ref[2 + parity, here] = value_s
-
-    lowest = group == levels // 2 - 1
-    highest = group == 0
-
-    def below(ref, k, edge_value=None):
-        if k % 2 == 0:
-            return ref[k + 1, here]
-        x = roll(ref[k - 1, here], -16, 1)
-        return x if edge_value is None else jnp.where(lowest, edge_value, x)
-
-    def above(ref, k, edge_value):
-        if k % 2 == 1:
-            return ref[k - 1, here]
-        return jnp.where(highest, edge_value, roll(ref[k + 1, here], 16, 1))
-
-    tracers = (
-        (ct, low_t, ae_t, an_t, au_t, hi_t, lo_t, up_t, dn_t, fe_t),
-        (cs, low_s, ae_s, an_s, au_s, hi_s, lo_s, up_s, dn_s, fe_s),
-    )
-    for strip in (0, 2):
-        ends = (strip, strip + 1)
-        tops = [[None, None], [None, None]]
-        for k in ends:
-            wet = cm[k, here]
-            east = low_and_anti(cu[k, here] * (wet * cm[k, to_east]))
-            north = low_and_anti(cv[k, here] * (wet * roll(wet, -1, 1)))
-            upward = low_and_anti(cw[k, here] * (wet * below(cm, k, 0.0)))
-            for n, (c, low, ae, an, au, hi, lo, _, _, face) in enumerate(tracers):
-                x = c[k, here]
-                fe, ae[k, here] = east(x, c[k, to_east])
-                fn, an[k, here] = north(x, roll(x, -1, 1))
-                fu, au[k, here] = upward(below(c, k), x)
-                face[k, here] = fe
-                tops[n][k % 2] = fu
-                low[k, here] = x - ((fe - face[k, to_west]) + (fn - roll(fn, 1, 1)) - fu)
-        for k in ends:
-            dry = cm[k, here] == 0.0
-            for n, (c, low, ae, an, au, hi, lo, _, _, _) in enumerate(tracers):
-                over = tops[n][0] if k % 2 == 1 else jnp.where(highest, 0.0, roll(tops[n][1], 16, 1))
-                x, lowered = c[k, here], low[k, here] - over
-                low[k, here] = lowered
-                hi[k, here] = jnp.where(dry, -BIG, jnp.maximum(x, lowered))
-                lo[k, here] = jnp.where(dry, BIG, jnp.minimum(x, lowered))
-        for k in ends:
-            for _, low, ae, an, au, hi, lo, rise, drop, _ in tracers:
-                top_value, low_value = hi[k, here], lo[k, here]
-                for x in (hi[k, to_east], hi[k, to_west], roll(top_value, -1, 1), roll(top_value, 1, 1),
-                          below(hi, k, -BIG), above(hi, k, -BIG)):
-                    top_value = jnp.maximum(top_value, x)
-                for x in (lo[k, to_east], lo[k, to_west], roll(low_value, -1, 1), roll(low_value, 1, 1),
-                          below(lo, k, BIG), above(lo, k, BIG)):
-                    low_value = jnp.minimum(low_value, x)
-                anti_n = an[k, here]
-                rise[k, here], drop[k, here] = ratios(
-                    low[k, here], top_value, low_value,
-                    (ae[k, to_west], roll(anti_n, 1, 1), au[k, here]), (ae[k, here], anti_n, above(au, k, 0.0)),
-                )
-        for k in ends:
-            for _, low, ae, an, au, hi, _, rise, drop, face in tracers:
-                r, d = rise[k, here], drop[k, here]
-                face[k, here] = limited(ae[k, here], r, d, rise[k, to_east], drop[k, to_east])
-                hi[k, here] = limited(au[k, here], below(rise, k), below(drop, k), r, d)
-        for k in ends:
-            for _, low, ae, an, au, hi, lo, rise, drop, face in tracers:
-                r, d = rise[k, here], drop[k, here]
-                fn = limited(an[k, here], r, d, roll(r, -1, 1), roll(d, -1, 1))
-                out = (face[k, here] - face[k, to_west]) + (fn - roll(fn, 1, 1))
-                lo[k, here] = low[k, here] - (out + (above(hi, k, 0.0) - hi[k, here]))
+                value = jnp.where(spot > 8, 0.0, value)
+            ref[parity, here] = value
+    strip_advection(scratch, levels, rows, lanes)
 
     _, _, place = lanes_of(rows, lanes)
-    ends = []
-    for tracer in tracers:
-        lo = tracer[6]
-        ends.append([
-            jnp.where(place < 6, lo[parity, OWN : OWN + rows], lo[2 + parity, OWN : OWN + rows])
-            for parity in range(2)
-        ])
+    ends = [
+        [jnp.where(place < 6, scratch[16 + n][parity, OWN : OWN + rows], south_end[n, parity]) for parity in range(2)]
+        for n in range(2)
+    ]
     lane, _, _ = lanes_of(rows, lanes)
     outer = (lane < 3) | (lane >= lanes - 3)
     solved = [None, None]
     for k in range(levels):
-        q, inv = number[k], inverse[k]
-        for n, adv in enumerate((adv_t, adv_s)):
-            x = jnp.where(outer, roll(ends[n][k % 2], -(16 * (k // 2) + 6), 1), adv[k])
-            if k > 0:
-                x = x + q * solved[n]
-            solved[n] = x * inv
-            (new_t, new_s)[n][k] = solved[n]
+        for n, (adv, out) in enumerate(((adv_t, new_t), (adv_s, new_s))):
+            x = jnp.where(outer, roll(ends[n][k % 2], -(16 * (k // 2) + 6), 1), adv[k]) * inverse[k]
+            solved[n] = x if k == 0 else x + onward[k] * solved[n]
+            out[k] = solved[n]
     for k in range(levels - 2, -1, -1):
-        ratio = number[k + 1] * inverse[k]
         for n, out in enumerate((new_t, new_s)):
-            solved[n] = out[k] + ratio * solved[n]
+            solved[n] = out[k] + back[k] * solved[n]
             out[k] = solved[n]
 
 
@@ -499,19 +543,24 @@
     def send(x, pairs):
         return lax.ppermute(x, AXES, pairs)
 
-    core, chip, chip1, bound, top, own, *held = call(
+    chip1, bound, top, own, *held = call(
         pack,
-        [(levels + 1, rows, lanes), (levels, rows, lanes), (16, lanes)] + [(2, rows, lanes)] * 2
-        + [(6, 2, rows, lanes)] + [jax.ShapeDtypeStruct(x.shape, x.dtype) for x in args],
+        [(16, lanes)] + [(2, rows, lanes)] * 2 + [(6, 2, rows, lanes)]
+        + [jax.ShapeDtypeStruct(x.shape, x.dtype) for x in args],
         [pltpu.with_memory_space_constraint(x, pltpu.HBM) for x in args],
         [pltpu.SemaphoreType.DMA((len(args),))],
     )
     chip1_in = send(chip1, inner)
+    core, chip = call(
+        pack_columns,
+        [(levels + 1, rows, lanes), (levels, rows, lanes)],
+        (*held[:5], *held[6:], bound, top),
+    )
     core_in = send(core, cores)
     chip_in = send(chip, chips)
     cell = (levels + 2, 40, lanes)
-    numbers, inverse, core_side, *cells = call(
-        prepare, [(levels, rows, lanes)] * 2 + [(2, rows, lanes)] + [cell] * 6, (*held, core_in)
+    inverse, onward, back, core_side, *cells = call(
+        prepare, [(levels, rows, lanes)] * 3 + [(2, rows, lanes)] + [cell] * 6, (*held, core_in)
     )
     fold, lat = call(repack, [(2 * wide + 8, lanes), (2 * wide, lanes)], (top, bound, core_in, chip1_in), limit=2)
     fold_in = send(fold, folds)
@@ -525,12 +574,18 @@
         limit=20,
         flops=20_000_000,
     )
-    strip = (4, 40, lanes)
+    strip = (2, 40, lanes)
+    south_in = call(
+        south,
+        [(2, 2, rows, lanes)],
+        (adv_t, own, core_side, chip_side, lat_in),
+        [(2, wide, lanes)] + [strip] * 24,
+    )[0]
     return call(
         finish,
         [(levels, rows, lanes)] * 2,
-        (adv_t, adv_s, numbers, inverse, own, core_side, chip_side, top, lat_in, fold_in),
-        [strip] * 6 + [(4, wide, lanes), (2, wide, lanes)] + [strip] * 18,
+        (adv_t, adv_s, inverse, onward, back, own, core_side, chip_side, top, lat_in, fold_in, south_in),
+        [(4, wide, lanes), (2, wide, lanes), (2, 2, rows, lanes)] + [strip] * 24,
     )
 
 

time: 20.4 us -> 20 us (0.980)
  Pallas kernels: 6.41 us -> 6.2 us
    pallas_call x5 -> x7, Pallas kernels: 6.41 us -> 6.2 us  [call(): pl.pallas_call(body, out_shape=tuple(outs), in_specs=[pl.BlockSpec(memory...]
  transfers between devices with their start and end apart: 5 -> 5, of which waited for: 2 -> 3; matrix products, arithmetic and copies ran while one was open for 0% -> 0% of each run, Pallas kernels for 14% -> 15%
where the time goes in v3:
time: 20 us; the launch traced here: 19.8 us
  starting transfers between devices  9.36 us (47%)
  Pallas kernels  6.2 us (31%)
  waiting for transfers between devices  3.54 us (18%)
  between operations  0.7 us (4%)
    ppermute x5, starting transfers between devices, send(): return lax.ppermute(x, AXES, pairs)  9.36 us
    pallas_call x7, Pallas kernels, call(): pl.pallas_call(body, out_shape=tuple(outs), in_specs=[pl.BlockSpec(memory...  6.2 us
    ppermute x5, waiting for transfers between devices, send(): return lax.ppermute(x, AXES, pairs)  3.54 us
  transfers between devices with their start and end apart: 5, of which 3 were waited for; matrix products, arithmetic and copies ran while one was open for 0% of the time, Pallas kernels for 15%

profile of v3, /device:TPU:0, one launch (start us, length us, event | category | flops | bytes accessed | tf_op | source)
XLA Modules:
  0.0 19.8 jit_solution(2762786676598464299)
XLA Ops:
  0.6 1.6 %shard_map.95 = (f32[16,128]{1,0:T(8,128)S(1)}, f32[2,16,128]{2,1,0:T(8,128)S(1)}, f32[2,16,128]{2,1,0:T(8,128)S(1)}, f32[6,2,16,128]{3,2,1,0:T(8,128)S(1)}, f32...) custom-call(f32[16,16,128]{2,1,0:T(8,128)} %t_any.1, ...), custom_call_target="tpu_custom_call" | custom-call | flops 2000000 | bytes 2000000 | tf_op jit(solution)/shard_map/pallas_call | solution.py:512
  2.3 0.1 shard_map.96
  2.4 0.6 %collective-permute-start = (f32[17,16,128]{2,1,0:T(8,128)S(1)}, f32[17,16,128]{2,1,0:T(8,128)S(1)}, u32[]{:S(2)}, u32[]{:S(2)}) collective-permute-start(f32[17,16,128]{2,1,0:T(8,128)S(1)} %get-tuple-element.41), channel_id=1, source_target_pairs={{0,2},{1,3},{2,0},{3,1},{4,6},{5,7},{6,4},{7,5},{8,10},{9,11},{10,... | collective-permute-start | bytes 417800 | tf_op jit(solution)/shard_map/ppermute | solution.py:544
  2.9 5.6 %collective-permute-start.1 = (f32[16,16,128]{2,1,0:T(8,128)S(1)}, f32[16,16,128]{2,1,0:T(8,128)S(1)}, u32[]{:S(2)}, u32[]{:S(2)}) collective-permute-start(f32[16,16,128]{2,1,0:T(8,128)S(1)} %get-tuple-element.48), channel_id=1, source_target_pairs={{0,30},{1,31},{2,4},{3,5},{4,2},{5,3},{6,8},{7,9},{8,6},{9,7},{10,... | collective-permute-start | bytes 393224 | tf_op jit(solution)/shard_map/ppermute | solution.py:544
  8.6 1.5 %collective-permute-start.2 = (f32[16,128]{1,0:T(8,128)S(1)}, f32[16,128]{1,0:T(8,128)S(1)}, u32[]{:S(2)}, u32[]{:S(2)}) collective-permute-start(f32[16,128]{1,0:T(8,128)S(1)} %get-tuple-element.57), channel_id=1, source_target_pairs={{2,4},{3,5},{4,2},{5,3},{6,8},{7,9},{8,6},{9,7},{10,12},{11,13},{1... | collective-permute-start | bytes 24584 | tf_op jit(solution)/shard_map/ppermute | solution.py:544
  10.1 2.1 %collective-permute-done.2.chip1 = f32[16,128]{1,0:T(8,128)S(1)} collective-permute-done((f32[16,128]{1,0:T(8,128)S(1)}, f32[16,128]{1,0:T(8,128)S(1)}, u32[]{:S(2)}, u32[]{:S(2)}) %collective-permute-start.2) | collective-permute-done | bytes 8224 | tf_op jit(solution)/shard_map/ppermute | solution.py:544
  12.2 0.0 collective-permute-done.core
  12.2 0.1 collective-permute-start.4
  12.3 1.6 %collective-permute-start.3 = (f32[48,128]{1,0:T(8,128)S(1)}, f32[48,128]{1,0:T(8,128)S(1)}, u32[]{:S(2)}, u32[]{:S(2)}) collective-permute-start(f32[48,128]{1,0:T(8,128)S(1)} %get-tuple-element.58), channel_id=1, source_target_pairs={{0,1},{1,0},{2,3},{3,2},{4,5},{5,4},{6,7},{7,6},{8,9},{9,8},{10,11... | collective-permute-start | bytes 73736 | tf_op jit(solution)/shard_map/ppermute | solution.py:544
  13.9 0.2 shard_map.97
  14.1 0.0 collective-permute-done.1.chip
  14.1 2.2 %shard_map.98 = (f32[16,16,128]{2,1,0:T(8,128)S(1)}, f32[16,16,128]{2,1,0:T(8,128)S(1)}, f32[2,16,128]{2,1,0:T(8,128)S(1)}, f32[18,40,128]{2,1,0:T(8,128)S(1)}, ...) custom-call(f32[18,40,128]{2,1,0:T(8,128)S(1)} %get-tuple-element.42, ...), custom_call_target="tpu_custom_call", output_to_operand_aliasing={{3}: (0, {}), {4}: (1, {}), {5}: (2, {}), {6}: (3, {}), {7}... | custom-call | flops 20000000 | bytes 2000000 | tf_op jit(solution)/shard_map/pallas_call | solution.py:512
  16.3 0.2 collective-permute-done.3.lat
  16.5 0.6 %shard_map.100.south_in = f32[2,2,16,128]{3,2,1,0:T(8,128)S(1)} custom-call(f32[16,16,128]{2,1,0:T(8,128)S(1)} %get-tuple-element.49.adv_t, f32[6,2,16,128]{3,2,1,0:T(8,128)S(1)} %get-tuple-element.54.own, f32[2,16,128]{2,1,0:T(8,128)S(1)} %get-tuple-element.55.core_side, f32[2,16,128]{2,1,0:T(8,128)S(1)} %get-tuple-element.56.chip_side, ...), custom_call_target="tpu_custom_call" | custom-call | flops 2000000 | bytes 2000000 | tf_op jit(solution)/shard_map/pallas_call | solution.py:512
  17.1 1.2 %collective-permute-done.4.fold = f32[56,128]{1,0:T(8,128)S(1)} collective-permute-done((f32[56,128]{1,0:T(8,128)S(1)}, f32[56,128]{1,0:T(8,128)S(1)}, u32[]{:S(2)}, u32[]{:S(2)}) %collective-permute-start.4) | collective-permute-done | bytes 28704 | tf_op jit(solution)/shard_map/ppermute | solution.py:544
  18.3 1.5 %shard_map.101 = (f32[16,16,128]{2,1,0:T(8,128)}, f32[16,16,128]{2,1,0:T(8,128)}) custom-call(f32[16,16,128]{2,1,0:T(8,128)S(1)} %get-tuple-element.49.adv_t, f32[16,16,128]{2,1,0:T(8,128)S(1)} %get-tuple-element.50.adv_s, f32[16,16,128]{2,1,0:T(8,128)S(1)} %get-tuple-element.51.inverse, f32[16,16,128]{2,1,0:T(8,128)S(1)} %get-tuple-element.52.onward, ...), custom_call_target="tpu_custom_call" | custom-call | flops 2000000 | bytes 2000000 | tf_op jit(solution)/shard_map/pallas_call | solution.py:512
  (1 shorter events, 0.0 us)
Async XLA Ops:
  2.4 9.8 %collective-permute-start = (f32[17,16,128]{2,1,0:T(8,128)S(1)}, f32[17,16,128]{2,1,0:T(8,128)S(1)}, u32[]{:S(2)}, u32[]{:S(2)}) collective-permute-start(f32[17,16,128]{2,1,0:T(8,128)S(1)} %get-tuple-element.41), channel_id=1, source_target_pairs={{0,2},{1,3},{2,0},{3,1},{4,6},{5,7},{6,4},{7,5},{8,10},{9,11},{10,... | collective-permute-start | bytes 417800 | tf_op jit(solution)/shard_map/ppermute | solution.py:544
  2.9 11.2 %collective-permute-start.1 = (f32[16,16,128]{2,1,0:T(8,128)S(1)}, f32[16,16,128]{2,1,0:T(8,128)S(1)}, u32[]{:S(2)}, u32[]{:S(2)}) collective-permute-start(f32[16,16,128]{2,1,0:T(8,128)S(1)} %get-tuple-element.48), channel_id=1, source_target_pairs={{0,30},{1,31},{2,4},{3,5},{4,2},{5,3},{6,8},{7,9},{8,6},{9,7},{10,... | collective-permute-start | bytes 393224 | tf_op jit(solution)/shard_map/ppermute | solution.py:544
  8.6 3.7 %collective-permute-start.2 = (f32[16,128]{1,0:T(8,128)S(1)}, f32[16,128]{1,0:T(8,128)S(1)}, u32[]{:S(2)}, u32[]{:S(2)}) collective-permute-start(f32[16,128]{1,0:T(8,128)S(1)} %get-tuple-element.57), channel_id=1, source_target_pairs={{2,4},{3,5},{4,2},{5,3},{6,8},{7,9},{8,6},{9,7},{10,12},{11,13},{1... | collective-permute-start | bytes 24584 | tf_op jit(solution)/shard_map/ppermute | solution.py:544
  12.2 6.1 %collective-permute-start.4 = (f32[56,128]{1,0:T(8,128)S(1)}, f32[56,128]{1,0:T(8,128)S(1)}, u32[]{:S(2)}, u32[]{:S(2)}) collective-permute-start(f32[56,128]{1,0:T(8,128)S(1)} %get-tuple-element.59), channel_id=1, source_target_pairs={{0,30},{1,31},{2,28},{3,29},{4,26},{5,27},{6,24},{7,25},{8,22},{9,... | collective-permute-start | bytes 86024 | tf_op jit(solution)/shard_map/ppermute | solution.py:544
  12.3 4.1 %collective-permute-start.3 = (f32[48,128]{1,0:T(8,128)S(1)}, f32[48,128]{1,0:T(8,128)S(1)}, u32[]{:S(2)}, u32[]{:S(2)}) collective-permute-start(f32[48,128]{1,0:T(8,128)S(1)} %get-tuple-element.58), channel_id=1, source_target_pairs={{0,1},{1,0},{2,3},{3,2},{4,5},{5,4},{6,7},{7,6},{8,9},{9,8},{10,11... | collective-permute-start | bytes 73736 | tf_op jit(solution)/shard_map/ppermute | solution.py:544

commit v4 on v3

--- a/solution.py
+++ b/solution.py
@@ -223,8 +223,11 @@
 
 
 def ratios(lowered, top_value, low_value, inward, outward):
-    gain = sum(jnp.maximum(x, 0.0) for x in inward) - sum(jnp.minimum(x, 0.0) for x in outward)
-    loss = gain + (sum(outward) - sum(inward))
+    (a, b, c), (x, y, z) = inward, outward
+    gain = (jnp.maximum(a, 0.0) + jnp.maximum(b, 0.0) + jnp.maximum(c, 0.0)) - (
+        jnp.minimum(x, 0.0) + jnp.minimum(y, 0.0) + jnp.minimum(z, 0.0)
+    )
+    loss = gain + ((x - a) + (y - b) + (z - c))
     rise = jnp.minimum(1.0, (top_value - lowered) / jnp.maximum(gain, FLUX_FLOOR))
     drop = jnp.minimum(1.0, (lowered - low_value) / jnp.maximum(loss, FLUX_FLOOR))
     return rise, drop
@@ -433,7 +436,7 @@
 
 def finish(
     adv_t, adv_s, inverse, onward, back, own, core_side, chip_side, top, lat, fold, south_in,
-    new_t, new_s, edge, mirror, south_end, *scratch,
+    out_t, out_s, edge, mirror, south_end, new_t, new_s, sems, *scratch,
 ):
     i, j = position()
     n_lon, n_lat = lax.axis_size("lon"), lax.axis_size("lat")
@@ -499,16 +502,31 @@
             x = jnp.where(outer, roll(ends[n][k % 2], -(16 * (k // 2) + 6), 1), adv[k]) * inverse[k]
             solved[n] = x if k == 0 else x + onward[k] * solved[n]
             out[k] = solved[n]
+    half = levels // 2
+    copies = []
+
+    def leave(start):
+        for held, out in ((new_t, out_t), (new_s, out_s)):
+            part = pl.ds(start, half)
+            copies.append(pltpu.make_async_copy(held.at[part], out.at[part], sems.at[len(copies)]))
+            copies[-1].start()
+
     for k in range(levels - 2, -1, -1):
         for n, out in enumerate((new_t, new_s)):
             solved[n] = out[k] + back[k] * solved[n]
             out[k] = solved[n]
+        if k == half:
+            leave(half)
+    leave(0)
+    for copy in copies:
+        copy.wait()
 
 
 def call(body, outs, args, scratch=(), aliases=None, limit=8, flops=2_000_000):
     vmem = pl.BlockSpec(memory_space=pltpu.VMEM)
     outs = [x if hasattr(x, "dtype") else jax.ShapeDtypeStruct(x, F32) for x in outs]
     where = pltpu.HBM if body is pack else pltpu.VMEM
+    vmem = pl.BlockSpec(memory_space=pltpu.HBM) if body is finish else vmem
     return pl.pallas_call(
         body,
         out_shape=tuple(outs),
@@ -585,7 +603,8 @@
         finish,
         [(levels, rows, lanes)] * 2,
         (adv_t, adv_s, inverse, onward, back, own, core_side, chip_side, top, lat_in, fold_in, south_in),
-        [(4, wide, lanes), (2, wide, lanes), (2, 2, rows, lanes)] + [strip] * 24,
+        [(4, wide, lanes), (2, wide, lanes), (2, 2, rows, lanes)] + [(levels, rows, lanes)] * 2
+        + [pltpu.SemaphoreType.DMA((4,))] + [strip] * 24,
     )
 
 

time: 20 us -> 20 us (level)
  no operation moved by 1% of the time
where the time goes in v4:
time: 20 us; the launch traced here: 19.8 us
  starting transfers between devices  9.36 us (47%)
  Pallas kernels  6.21 us (31%)
  waiting for transfers between devices  3.54 us (18%)
  between operations  0.7 us (4%)
    ppermute x5, starting transfers between devices, send(): return lax.ppermute(x, AXES, pairs)  9.36 us
    pallas_call x7, Pallas kernels, call(): pl.pallas_call(body, out_shape=tuple(outs), in_specs=[pl.BlockSpec(memory...  6.21 us
    ppermute x5, waiting for transfers between devices, send(): return lax.ppermute(x, AXES, pairs)  3.54 us
  transfers between devices with their start and end apart: 5, of which 3 were waited for; matrix products, arithmetic and copies ran while one was open for 0% of the time, Pallas kernels for 15%

profile of v4, /device:TPU:0, one launch (start us, length us, event | category | flops | bytes accessed | tf_op | source)
XLA Modules:
  0.0 19.8 jit_solution(2953702128710633761)
XLA Ops:
  0.6 1.6 %shard_map.95 = (f32[16,128]{1,0:T(8,128)S(1)}, f32[2,16,128]{2,1,0:T(8,128)S(1)}, f32[2,16,128]{2,1,0:T(8,128)S(1)}, f32[6,2,16,128]{3,2,1,0:T(8,128)S(1)}, f32...) custom-call(f32[16,16,128]{2,1,0:T(8,128)} %t_any.1, ...), custom_call_target="tpu_custom_call" | custom-call | flops 2000000 | bytes 2000000 | tf_op jit(solution)/shard_map/pallas_call | solution.py:530
  2.3 0.1 shard_map.96
  2.4 0.6 %collective-permute-start = (f32[17,16,128]{2,1,0:T(8,128)S(1)}, f32[17,16,128]{2,1,0:T(8,128)S(1)}, u32[]{:S(2)}, u32[]{:S(2)}) collective-permute-start(f32[17,16,128]{2,1,0:T(8,128)S(1)} %get-tuple-element.41), channel_id=1, source_target_pairs={{0,2},{1,3},{2,0},{3,1},{4,6},{5,7},{6,4},{7,5},{8,10},{9,11},{10,... | collective-permute-start | bytes 417800 | tf_op jit(solution)/shard_map/ppermute | solution.py:562
  2.9 5.6 %collective-permute-start.1 = (f32[16,16,128]{2,1,0:T(8,128)S(1)}, f32[16,16,128]{2,1,0:T(8,128)S(1)}, u32[]{:S(2)}, u32[]{:S(2)}) collective-permute-start(f32[16,16,128]{2,1,0:T(8,128)S(1)} %get-tuple-element.48), channel_id=1, source_target_pairs={{0,30},{1,31},{2,4},{3,5},{4,2},{5,3},{6,8},{7,9},{8,6},{9,7},{10,... | collective-permute-start | bytes 393224 | tf_op jit(solution)/shard_map/ppermute | solution.py:562
  8.6 1.5 %collective-permute-start.2 = (f32[16,128]{1,0:T(8,128)S(1)}, f32[16,128]{1,0:T(8,128)S(1)}, u32[]{:S(2)}, u32[]{:S(2)}) collective-permute-start(f32[16,128]{1,0:T(8,128)S(1)} %get-tuple-element.57), channel_id=1, source_target_pairs={{2,4},{3,5},{4,2},{5,3},{6,8},{7,9},{8,6},{9,7},{10,12},{11,13},{1... | collective-permute-start | bytes 24584 | tf_op jit(solution)/shard_map/ppermute | solution.py:562
  10.1 2.1 %collective-permute-done.2.chip1 = f32[16,128]{1,0:T(8,128)S(1)} collective-permute-done((f32[16,128]{1,0:T(8,128)S(1)}, f32[16,128]{1,0:T(8,128)S(1)}, u32[]{:S(2)}, u32[]{:S(2)}) %collective-permute-start.2) | collective-permute-done | bytes 8224 | tf_op jit(solution)/shard_map/ppermute | solution.py:562
  12.2 0.0 collective-permute-done.core
  12.2 0.1 collective-permute-start.4
  12.3 1.6 %collective-permute-start.3 = (f32[48,128]{1,0:T(8,128)S(1)}, f32[48,128]{1,0:T(8,128)S(1)}, u32[]{:S(2)}, u32[]{:S(2)}) collective-permute-start(f32[48,128]{1,0:T(8,128)S(1)} %get-tuple-element.58), channel_id=1, source_target_pairs={{0,1},{1,0},{2,3},{3,2},{4,5},{5,4},{6,7},{7,6},{8,9},{9,8},{10,11... | collective-permute-start | bytes 73736 | tf_op jit(solution)/shard_map/ppermute | solution.py:562
  13.9 0.2 shard_map.97
  14.1 0.0 collective-permute-done.1.chip
  14.1 2.2 %shard_map.98 = (f32[16,16,128]{2,1,0:T(8,128)S(1)}, f32[16,16,128]{2,1,0:T(8,128)S(1)}, f32[2,16,128]{2,1,0:T(8,128)S(1)}, f32[18,40,128]{2,1,0:T(8,128)S(1)}, ...) custom-call(f32[18,40,128]{2,1,0:T(8,128)S(1)} %get-tuple-element.42, ...), custom_call_target="tpu_custom_call", output_to_operand_aliasing={{3}: (0, {}), {4}: (1, {}), {5}: (2, {}), {6}: (3, {}), {7}... | custom-call | flops 20000000 | bytes 2000000 | tf_op jit(solution)/shard_map/pallas_call | solution.py:530
  16.3 0.2 collective-permute-done.3.lat
  16.5 0.6 %shard_map.100.south_in = f32[2,2,16,128]{3,2,1,0:T(8,128)S(1)} custom-call(f32[16,16,128]{2,1,0:T(8,128)S(1)} %get-tuple-element.49.adv_t, f32[6,2,16,128]{3,2,1,0:T(8,128)S(1)} %get-tuple-element.54.own, f32[2,16,128]{2,1,0:T(8,128)S(1)} %get-tuple-element.55.core_side, f32[2,16,128]{2,1,0:T(8,128)S(1)} %get-tuple-element.56.chip_side, ...), custom_call_target="tpu_custom_call" | custom-call | flops 2000000 | bytes 2000000 | tf_op jit(solution)/shard_map/pallas_call | solution.py:530
  17.1 1.2 %collective-permute-done.4.fold = f32[56,128]{1,0:T(8,128)S(1)} collective-permute-done((f32[56,128]{1,0:T(8,128)S(1)}, f32[56,128]{1,0:T(8,128)S(1)}, u32[]{:S(2)}, u32[]{:S(2)}) %collective-permute-start.4) | collective-permute-done | bytes 28704 | tf_op jit(solution)/shard_map/ppermute | solution.py:562
  18.3 1.5 %shard_map.101 = (f32[16,16,128]{2,1,0:T(8,128)}, f32[16,16,128]{2,1,0:T(8,128)}) custom-call(f32[16,16,128]{2,1,0:T(8,128)S(1)} %get-tuple-element.49.adv_t, f32[16,16,128]{2,1,0:T(8,128)S(1)} %get-tuple-element.50.adv_s, f32[16,16,128]{2,1,0:T(8,128)S(1)} %get-tuple-element.51.inverse, f32[16,16,128]{2,1,0:T(8,128)S(1)} %get-tuple-element.52.onward, ...), custom_call_target="tpu_custom_call" | custom-call | flops 2000000 | bytes 2000000 | tf_op jit(solution)/shard_map/pallas_call | solution.py:530
  (1 shorter events, 0.0 us)
Async XLA Ops:
  2.4 9.8 %collective-permute-start = (f32[17,16,128]{2,1,0:T(8,128)S(1)}, f32[17,16,128]{2,1,0:T(8,128)S(1)}, u32[]{:S(2)}, u32[]{:S(2)}) collective-permute-start(f32[17,16,128]{2,1,0:T(8,128)S(1)} %get-tuple-element.41), channel_id=1, source_target_pairs={{0,2},{1,3},{2,0},{3,1},{4,6},{5,7},{6,4},{7,5},{8,10},{9,11},{10,... | collective-permute-start | bytes 417800 | tf_op jit(solution)/shard_map/ppermute | solution.py:562
  2.9 11.2 %collective-permute-start.1 = (f32[16,16,128]{2,1,0:T(8,128)S(1)}, f32[16,16,128]{2,1,0:T(8,128)S(1)}, u32[]{:S(2)}, u32[]{:S(2)}) collective-permute-start(f32[16,16,128]{2,1,0:T(8,128)S(1)} %get-tuple-element.48), channel_id=1, source_target_pairs={{0,30},{1,31},{2,4},{3,5},{4,2},{5,3},{6,8},{7,9},{8,6},{9,7},{10,... | collective-permute-start | bytes 393224 | tf_op jit(solution)/shard_map/ppermute | solution.py:562
  8.6 3.7 %collective-permute-start.2 = (f32[16,128]{1,0:T(8,128)S(1)}, f32[16,128]{1,0:T(8,128)S(1)}, u32[]{:S(2)}, u32[]{:S(2)}) collective-permute-start(f32[16,128]{1,0:T(8,128)S(1)} %get-tuple-element.57), channel_id=1, source_target_pairs={{2,4},{3,5},{4,2},{5,3},{6,8},{7,9},{8,6},{9,7},{10,12},{11,13},{1... | collective-permute-start | bytes 24584 | tf_op jit(solution)/shard_map/ppermute | solution.py:562
  12.2 6.1 %collective-permute-start.4 = (f32[56,128]{1,0:T(8,128)S(1)}, f32[56,128]{1,0:T(8,128)S(1)}, u32[]{:S(2)}, u32[]{:S(2)}) collective-permute-start(f32[56,128]{1,0:T(8,128)S(1)} %get-tuple-element.59), channel_id=1, source_target_pairs={{0,30},{1,31},{2,28},{3,29},{4,26},{5,27},{6,24},{7,25},{8,22},{9,... | collective-permute-start | bytes 86024 | tf_op jit(solution)/shard_map/ppermute | solution.py:562
  12.3 4.1 %collective-permute-start.3 = (f32[48,128]{1,0:T(8,128)S(1)}, f32[48,128]{1,0:T(8,128)S(1)}, u32[]{:S(2)}, u32[]{:S(2)}) collective-permute-start(f32[48,128]{1,0:T(8,128)S(1)} %get-tuple-element.58), channel_id=1, source_target_pairs={{0,1},{1,0},{2,3},{3,2},{4,5},{5,4},{6,7},{7,6},{8,9},{9,8},{10,11... | collective-permute-start | bytes 73736 | tf_op jit(solution)/shard_map/ppermute | solution.py:562

commit v5 on v4

--- a/solution.py
+++ b/solution.py
@@ -392,8 +392,8 @@
             lo[k, here] = low[k, here] - (out + (above(hi, k, 0.0) - hi[k, here]))
 
 
-def strip_cells(scratch, own, core_side, chip_side):
-    cells, rows = scratch[:6], own.shape[2]
+def strip_cells(cells, own, core_side, chip_side):
+    rows = own.shape[2]
     for n, ref in enumerate(cells):
         for parity in range(2):
             ref[parity, OWN : OWN + rows] = own[n, parity]
@@ -408,16 +408,15 @@
     by_parity(fill)
 
 
-def south_strip(scratch, own, core_side, chip_side, edge, levels, out):
-    rows, lanes = own.shape[2:]
+def south_strip(scratch, both, edge, levels, out):
+    rows, lanes = out.shape[2:]
     wide = rows + 8
     _, _, spot = lanes_of(wide, lanes)
     _, j = position()
     here = pl.ds(8, wide)
-    strip_cells(scratch, own, core_side, chip_side)
-    for parity in range(2):
-        for ref, (name, start, count) in zip(scratch, SPOTS):
-            value = jnp.where(spot < 6, roll(edge[parity], 6 - count - start, 1), ref[parity, here])
+    for parity in range(2):
+        for ref, mine, (name, start, count) in zip(scratch, both, SPOTS):
+            value = jnp.where(spot < 6, roll(edge[parity], 6 - count - start, 1), mine[parity, here])
             if name == "m":
                 value = jnp.where((spot < 3) | (spot > 11) | ((spot < 6) & (j == 0)), 0.0, value)
             ref[parity, here] = value
@@ -427,15 +426,17 @@
             out[n, parity] = scratch[16 + n][parity, OWN : OWN + rows]
 
 
-def south(adv_t, own, core_side, chip_side, lat, out, edge, *scratch):
+def south(adv_t, own, core_side, chip_side, lat, out, *rest):
     levels, rows, _ = adv_t.shape
+    both, edge, scratch = rest[:6], rest[6], rest[7:]
+    strip_cells(both, own, core_side, chip_side)
     for parity in range(2):
         edge[parity] = lat[(rows + 8) * parity : (rows + 8) * (parity + 1)]
-    south_strip(scratch, own, core_side, chip_side, edge, levels, out)
+    south_strip(scratch, both, edge, levels, out)
 
 
 def finish(
-    adv_t, adv_s, inverse, onward, back, own, core_side, chip_side, top, lat, fold, south_in,
+    adv_t, adv_s, inverse, onward, back, top, lat, fold, south_in, bt, bs, bu, bv, bw, bm,
     out_t, out_s, edge, mirror, south_end, new_t, new_s, sems, *scratch,
 ):
     i, j = position()
@@ -445,6 +446,7 @@
     wide = rows + 8
     _, _, spot = lanes_of(wide, lanes)
     here = pl.ds(8, wide)
+    both = (bt, bs, bu, bv, bw, bm)
 
     for parity in range(2):
         edge[parity] = lat[wide * parity : wide * parity + wide]
@@ -465,21 +467,20 @@
 
     @pl.when((first | last) & (j > 0))
     def _():
-        south_strip(scratch, own, core_side, chip_side, edge, levels, south_end)
+        south_strip(scratch, both, edge, levels, south_end)
 
     for parity in range(2):
         for r in range(wide):
             q = wide - 1 - r
             mirror[parity, r : r + 1] = edge[2 + parity, q : q + 1]
 
-    strip_cells(scratch, own, core_side, chip_side)
     _, u_start, u_count = SPOTS[2]
     for parity in range(2):
         other, mir = edge[parity], mirror[parity]
         mir = jnp.where((spot >= u_start) & (spot < u_start + u_count), roll(mir, -1, 0), mir)
         source = jnp.where(is_top, mir, other)
-        for ref, (name, start, count) in zip(scratch, SPOTS):
-            mine = ref[parity, here]
+        for ref, held, (name, start, count) in zip(scratch, both, SPOTS):
+            mine = held[parity, here]
             value = jnp.where(spot < 6, mine, roll(source, 6 - start, 1))
             if name == "v":
                 folded = 0.5 * (mine + roll(source, 5 - (start + 2), 1))
@@ -593,16 +594,16 @@
         flops=20_000_000,
     )
     strip = (2, 40, lanes)
-    south_in = call(
+    south_in, *both = call(
         south,
-        [(2, 2, rows, lanes)],
+        [(2, 2, rows, lanes)] + [strip] * 6,
         (adv_t, own, core_side, chip_side, lat_in),
         [(2, wide, lanes)] + [strip] * 24,
-    )[0]
+    )
     return call(
         finish,
         [(levels, rows, lanes)] * 2,
-        (adv_t, adv_s, inverse, onward, back, own, core_side, chip_side, top, lat_in, fold_in, south_in),
+        (adv_t, adv_s, inverse, onward, back, top, lat_in, fold_in, south_in, *both),
         [(4, wide, lanes), (2, wide, lanes), (2, 2, rows, lanes)] + [(levels, rows, lanes)] * 2
         + [pltpu.SemaphoreType.DMA((4,))] + [strip] * 24,
     )

time: 20 us -> 20 us (level)
  no operation moved by 1% of the time
where the time goes in v5:
time: 20 us; the launch traced here: 19.8 us
  starting transfers between devices  9.36 us (47%)
  Pallas kernels  6.19 us (31%)
  waiting for transfers between devices  3.55 us (18%)
  between operations  0.7 us (4%)
    ppermute x5, starting transfers between devices, send(): return lax.ppermute(x, AXES, pairs)  9.36 us
    pallas_call x7, Pallas kernels, call(): pl.pallas_call(body, out_shape=tuple(outs), in_specs=[pl.BlockSpec(memory...  6.19 us
    ppermute x5, waiting for transfers between devices, send(): return lax.ppermute(x, AXES, pairs)  3.55 us
  transfers between devices with their start and end apart: 5, of which 3 were waited for; matrix products, arithmetic and copies ran while one was open for 0% of the time, Pallas kernels for 15%

profile of v5, /device:TPU:0, one launch (start us, length us, event | category | flops | bytes accessed | tf_op | source)
XLA Modules:
  0.0 19.8 jit_solution(11884632169387037349)
XLA Ops:
  0.6 1.6 %shard_map.95 = (f32[16,128]{1,0:T(8,128)S(1)}, f32[2,16,128]{2,1,0:T(8,128)S(1)}, f32[2,16,128]{2,1,0:T(8,128)S(1)}, f32[6,2,16,128]{3,2,1,0:T(8,128)S(1)}, f32...) custom-call(f32[16,16,128]{2,1,0:T(8,128)} %t_any.1, ...), custom_call_target="tpu_custom_call" | custom-call | flops 2000000 | bytes 2000000 | tf_op jit(solution)/shard_map/pallas_call | solution.py:531
  2.3 0.1 shard_map.96
  2.4 0.6 %collective-permute-start = (f32[17,16,128]{2,1,0:T(8,128)S(1)}, f32[17,16,128]{2,1,0:T(8,128)S(1)}, u32[]{:S(2)}, u32[]{:S(2)}) collective-permute-start(f32[17,16,128]{2,1,0:T(8,128)S(1)} %get-tuple-element.48), channel_id=1, source_target_pairs={{0,2},{1,3},{2,0},{3,1},{4,6},{5,7},{6,4},{7,5},{8,10},{9,11},{10,... | collective-permute-start | bytes 417800 | tf_op jit(solution)/shard_map/ppermute | solution.py:563
  2.9 5.6 %collective-permute-start.1 = (f32[16,16,128]{2,1,0:T(8,128)S(1)}, f32[16,16,128]{2,1,0:T(8,128)S(1)}, u32[]{:S(2)}, u32[]{:S(2)}) collective-permute-start(f32[16,16,128]{2,1,0:T(8,128)S(1)} %get-tuple-element.55), channel_id=1, source_target_pairs={{0,30},{1,31},{2,4},{3,5},{4,2},{5,3},{6,8},{7,9},{8,6},{9,7},{10,... | collective-permute-start | bytes 393224 | tf_op jit(solution)/shard_map/ppermute | solution.py:563
  8.6 1.5 %collective-permute-start.2 = (f32[16,128]{1,0:T(8,128)S(1)}, f32[16,128]{1,0:T(8,128)S(1)}, u32[]{:S(2)}, u32[]{:S(2)}) collective-permute-start(f32[16,128]{1,0:T(8,128)S(1)} %get-tuple-element.61), channel_id=1, source_target_pairs={{2,4},{3,5},{4,2},{5,3},{6,8},{7,9},{8,6},{9,7},{10,12},{11,13},{1... | collective-permute-start | bytes 24584 | tf_op jit(solution)/shard_map/ppermute | solution.py:563
  10.1 2.1 %collective-permute-done.2.chip1 = f32[16,128]{1,0:T(8,128)S(1)} collective-permute-done((f32[16,128]{1,0:T(8,128)S(1)}, f32[16,128]{1,0:T(8,128)S(1)}, u32[]{:S(2)}, u32[]{:S(2)}) %collective-permute-start.2) | collective-permute-done | bytes 8224 | tf_op jit(solution)/shard_map/ppermute | solution.py:563
  12.2 0.0 collective-permute-done.core
  12.2 0.1 collective-permute-start.4
  12.3 1.6 %collective-permute-start.3 = (f32[48,128]{1,0:T(8,128)S(1)}, f32[48,128]{1,0:T(8,128)S(1)}, u32[]{:S(2)}, u32[]{:S(2)}) collective-permute-start(f32[48,128]{1,0:T(8,128)S(1)} %get-tuple-element.62), channel_id=1, source_target_pairs={{0,1},{1,0},{2,3},{3,2},{4,5},{5,4},{6,7},{7,6},{8,9},{9,8},{10,11... | collective-permute-start | bytes 73736 | tf_op jit(solution)/shard_map/ppermute | solution.py:563
  13.9 0.2 shard_map.97
  14.1 0.0 collective-permute-done.1.chip
  14.1 2.2 %shard_map.98 = (f32[16,16,128]{2,1,0:T(8,128)S(1)}, f32[16,16,128]{2,1,0:T(8,128)S(1)}, f32[2,16,128]{2,1,0:T(8,128)S(1)}, f32[18,40,128]{2,1,0:T(8,128)S(1)}, ...) custom-call(f32[18,40,128]{2,1,0:T(8,128)S(1)} %get-tuple-element.49, ...), custom_call_target="tpu_custom_call", output_to_operand_aliasing={{3}: (0, {}), {4}: (1, {}), {5}: (2, {}), {6}: (3, {}), {7}... | custom-call | flops 20000000 | bytes 2000000 | tf_op jit(solution)/shard_map/pallas_call | solution.py:531
  16.3 0.2 collective-permute-done.3.lat
  16.5 0.6 %shard_map.100 = (f32[2,2,16,128]{3,2,1,0:T(8,128)S(1)}, f32[2,40,128]{2,1,0:T(8,128)S(1)}, f32[2,40,128]{2,1,0:T(8,128)S(1)}, f32[2,40,128]{2,1,0:T(8,128)S(1)}...) custom-call(f32[16,16,128]{2,1,0:T(8,128)S(1)} %get-tuple-element.56.adv_t, ...), custom_call_target="tpu_custom_call" | custom-call | flops 2000000 | bytes 2000000 | tf_op jit(solution)/shard_map/pallas_call | solution.py:531
  17.1 1.2 %collective-permute-done.4.fold = f32[56,128]{1,0:T(8,128)S(1)} collective-permute-done((f32[56,128]{1,0:T(8,128)S(1)}, f32[56,128]{1,0:T(8,128)S(1)}, u32[]{:S(2)}, u32[]{:S(2)}) %collective-permute-start.4) | collective-permute-done | bytes 28704 | tf_op jit(solution)/shard_map/ppermute | solution.py:563
  18.3 1.5 %shard_map.101 = (f32[16,16,128]{2,1,0:T(8,128)}, f32[16,16,128]{2,1,0:T(8,128)}) custom-call(f32[16,16,128]{2,1,0:T(8,128)S(1)} %get-tuple-element.56.adv_t, f32[16,16,128]{2,1,0:T(8,128)S(1)} %get-tuple-element.57.adv_s, f32[16,16,128]{2,1,0:T(8,128)S(1)} %get-tuple-element.58.inverse, f32[16,16,128]{2,1,0:T(8,128)S(1)} %get-tuple-element.59.onward, ...), custom_call_target="tpu_custom_call" | custom-call | flops 2000000 | bytes 2000000 | tf_op jit(solution)/shard_map/pallas_call | solution.py:531
  (1 shorter events, 0.0 us)
Async XLA Ops:
  2.4 9.8 %collective-permute-start = (f32[17,16,128]{2,1,0:T(8,128)S(1)}, f32[17,16,128]{2,1,0:T(8,128)S(1)}, u32[]{:S(2)}, u32[]{:S(2)}) collective-permute-start(f32[17,16,128]{2,1,0:T(8,128)S(1)} %get-tuple-element.48), channel_id=1, source_target_pairs={{0,2},{1,3},{2,0},{3,1},{4,6},{5,7},{6,4},{7,5},{8,10},{9,11},{10,... | collective-permute-start | bytes 417800 | tf_op jit(solution)/shard_map/ppermute | solution.py:563
  2.9 11.2 %collective-permute-start.1 = (f32[16,16,128]{2,1,0:T(8,128)S(1)}, f32[16,16,128]{2,1,0:T(8,128)S(1)}, u32[]{:S(2)}, u32[]{:S(2)}) collective-permute-start(f32[16,16,128]{2,1,0:T(8,128)S(1)} %get-tuple-element.55), channel_id=1, source_target_pairs={{0,30},{1,31},{2,4},{3,5},{4,2},{5,3},{6,8},{7,9},{8,6},{9,7},{10,... | collective-permute-start | bytes 393224 | tf_op jit(solution)/shard_map/ppermute | solution.py:563
  8.6 3.7 %collective-permute-start.2 = (f32[16,128]{1,0:T(8,128)S(1)}, f32[16,128]{1,0:T(8,128)S(1)}, u32[]{:S(2)}, u32[]{:S(2)}) collective-permute-start(f32[16,128]{1,0:T(8,128)S(1)} %get-tuple-element.61), channel_id=1, source_target_pairs={{2,4},{3,5},{4,2},{5,3},{6,8},{7,9},{8,6},{9,7},{10,12},{11,13},{1... | collective-permute-start | bytes 24584 | tf_op jit(solution)/shard_map/ppermute | solution.py:563
  12.2 6.1 %collective-permute-start.4 = (f32[56,128]{1,0:T(8,128)S(1)}, f32[56,128]{1,0:T(8,128)S(1)}, u32[]{:S(2)}, u32[]{:S(2)}) collective-permute-start(f32[56,128]{1,0:T(8,128)S(1)} %get-tuple-element.63), channel_id=1, source_target_pairs={{0,30},{1,31},{2,28},{3,29},{4,26},{5,27},{6,24},{7,25},{8,22},{9,... | collective-permute-start | bytes 86024 | tf_op jit(solution)/shard_map/ppermute | solution.py:563
  12.3 4.1 %collective-permute-start.3 = (f32[48,128]{1,0:T(8,128)S(1)}, f32[48,128]{1,0:T(8,128)S(1)}, u32[]{:S(2)}, u32[]{:S(2)}) collective-permute-start(f32[48,128]{1,0:T(8,128)S(1)} %get-tuple-element.62), channel_id=1, source_target_pairs={{0,1},{1,0},{2,3},{3,2},{4,5},{5,4},{6,7},{7,6},{8,9},{9,8},{10,11... | collective-permute-start | bytes 73736 | tf_op jit(solution)/shard_map/ppermute | solution.py:563

commit v6 on v5

--- a/solution.py
+++ b/solution.py
@@ -183,8 +183,8 @@
         out[parity] = x
 
 
-def prepare(t, s, u, v, w, dc, flag, depth, core, inverse, onward, back, core_side, ct, cs, cu, cv, cw, cm):
-    levels, rows, lanes = t.shape
+def prepare(t, s, u, v, w, dc, flag, depth, core, inverse, onward, back, ct, cs, cu, cv, cw, cm):
+    levels, rows, _ = t.shape
     flags, depths = flag[...], depth[...]
     zero = jnp.zeros(flags.shape, F32)
     q = [zero]
@@ -209,7 +209,6 @@
         cv[k + 1, OWN : OWN + rows] = v[k]
         cw[k + 1, OWN : OWN + rows] = w[k] if k < levels - 1 else zero
         cm[k + 1, OWN : OWN + rows] = wet_of(flags, depths, k)
-    at_strips(core, core_side, levels, rows, lanes)
     by_parity(lambda even: columns(core, even, (ct, cs, cu, cv, cw, cm), levels, rows))
 
 
@@ -426,9 +425,10 @@
             out[n, parity] = scratch[16 + n][parity, OWN : OWN + rows]
 
 
-def south(adv_t, own, core_side, chip_side, lat, out, *rest):
-    levels, rows, _ = adv_t.shape
-    both, edge, scratch = rest[:6], rest[6], rest[7:]
+def south(adv_t, own, core, chip_side, lat, out, *rest):
+    levels, rows, lanes = adv_t.shape
+    both, edge, core_side, scratch = rest[:6], rest[6], rest[7], rest[8:]
+    at_strips(core, core_side, levels, rows, lanes)
     strip_cells(both, own, core_side, chip_side)
     for parity in range(2):
         edge[parity] = lat[(rows + 8) * parity : (rows + 8) * (parity + 1)]
@@ -578,8 +578,8 @@
     core_in = send(core, cores)
     chip_in = send(chip, chips)
     cell = (levels + 2, 40, lanes)
-    inverse, onward, back, core_side, *cells = call(
-        prepare, [(levels, rows, lanes)] * 3 + [(2, rows, lanes)] + [cell] * 6, (*held, core_in)
+    inverse, onward, back, *cells = call(
+        prepare, [(levels, rows, lanes)] * 3 + [cell] * 6, (*held, core_in)
     )
     fold, lat = call(repack, [(2 * wide + 8, lanes), (2 * wide, lanes)], (top, bound, core_in, chip1_in), limit=2)
     fold_in = send(fold, folds)
@@ -597,8 +597,8 @@
     south_in, *both = call(
         south,
         [(2, 2, rows, lanes)] + [strip] * 6,
-        (adv_t, own, core_side, chip_side, lat_in),
-        [(2, wide, lanes)] + [strip] * 24,
+        (adv_t, own, core_in, chip_side, lat_in),
+        [(2, wide, lanes), (2, rows, lanes)] + [strip] * 24,
     )
     return call(
         finish,

time: 20 us -> 20 us (level)
  no operation moved by 1% of the time
where the time goes in v6:
time: 20 us; the launch traced here: 19.8 us
  starting transfers between devices  9.36 us (47%)
  Pallas kernels  6.27 us (31%)
  waiting for transfers between devices  3.47 us (17%)
  between operations  0.7 us (4%)
    ppermute x5, starting transfers between devices, send(): return lax.ppermute(x, AXES, pairs)  9.36 us
    pallas_call x7, Pallas kernels, call(): pl.pallas_call(body, out_shape=tuple(outs), in_specs=[pl.BlockSpec(memory...  6.27 us
    ppermute x5, waiting for transfers between devices, send(): return lax.ppermute(x, AXES, pairs)  3.47 us
  transfers between devices with their start and end apart: 5, of which 3 were waited for; matrix products, arithmetic and copies ran while one was open for 0% of the time, Pallas kernels for 15%

profile of v6, /device:TPU:0, one launch (start us, length us, event | category | flops | bytes accessed | tf_op | source)
XLA Modules:
  0.0 19.8 jit_solution(7864855689615029511)
XLA Ops:
  0.6 1.6 %shard_map.95 = (f32[16,128]{1,0:T(8,128)S(1)}, f32[2,16,128]{2,1,0:T(8,128)S(1)}, f32[2,16,128]{2,1,0:T(8,128)S(1)}, f32[6,2,16,128]{3,2,1,0:T(8,128)S(1)}, f32...) custom-call(f32[16,16,128]{2,1,0:T(8,128)} %t_any.1, ...), custom_call_target="tpu_custom_call" | custom-call | flops 2000000 | bytes 2000000 | tf_op jit(solution)/shard_map/pallas_call | solution.py:531
  2.3 0.1 shard_map.96
  2.4 0.6 %collective-permute-start = (f32[17,16,128]{2,1,0:T(8,128)S(1)}, f32[17,16,128]{2,1,0:T(8,128)S(1)}, u32[]{:S(2)}, u32[]{:S(2)}) collective-permute-start(f32[17,16,128]{2,1,0:T(8,128)S(1)} %get-tuple-element.47), channel_id=1, source_target_pairs={{0,2},{1,3},{2,0},{3,1},{4,6},{5,7},{6,4},{7,5},{8,10},{9,11},{10,... | collective-permute-start | bytes 417800 | tf_op jit(solution)/shard_map/ppermute | solution.py:563
  2.9 5.6 %collective-permute-start.1 = (f32[16,16,128]{2,1,0:T(8,128)S(1)}, f32[16,16,128]{2,1,0:T(8,128)S(1)}, u32[]{:S(2)}, u32[]{:S(2)}) collective-permute-start(f32[16,16,128]{2,1,0:T(8,128)S(1)} %get-tuple-element.54), channel_id=1, source_target_pairs={{0,30},{1,31},{2,4},{3,5},{4,2},{5,3},{6,8},{7,9},{8,6},{9,7},{10,... | collective-permute-start | bytes 393224 | tf_op jit(solution)/shard_map/ppermute | solution.py:563
  8.6 1.5 %collective-permute-start.2 = (f32[16,128]{1,0:T(8,128)S(1)}, f32[16,128]{1,0:T(8,128)S(1)}, u32[]{:S(2)}, u32[]{:S(2)}) collective-permute-start(f32[16,128]{1,0:T(8,128)S(1)} %get-tuple-element.60), channel_id=1, source_target_pairs={{2,4},{3,5},{4,2},{5,3},{6,8},{7,9},{8,6},{9,7},{10,12},{11,13},{1... | collective-permute-start | bytes 24584 | tf_op jit(solution)/shard_map/ppermute | solution.py:563
  10.1 2.1 %collective-permute-done.2.chip1 = f32[16,128]{1,0:T(8,128)S(1)} collective-permute-done((f32[16,128]{1,0:T(8,128)S(1)}, f32[16,128]{1,0:T(8,128)S(1)}, u32[]{:S(2)}, u32[]{:S(2)}) %collective-permute-start.2) | collective-permute-done | bytes 8224 | tf_op jit(solution)/shard_map/ppermute | solution.py:563
  12.2 0.0 collective-permute-done.core
  12.2 0.1 collective-permute-start.4
  12.3 1.6 %collective-permute-start.3 = (f32[48,128]{1,0:T(8,128)S(1)}, f32[48,128]{1,0:T(8,128)S(1)}, u32[]{:S(2)}, u32[]{:S(2)}) collective-permute-start(f32[48,128]{1,0:T(8,128)S(1)} %get-tuple-element.61), channel_id=1, source_target_pairs={{0,1},{1,0},{2,3},{3,2},{4,5},{5,4},{6,7},{7,6},{8,9},{9,8},{10,11... | collective-permute-start | bytes 73736 | tf_op jit(solution)/shard_map/ppermute | solution.py:563
  13.9 0.2 shard_map.97
  14.1 0.0 collective-permute-done.1.chip
  14.1 2.2 %shard_map.98 = (f32[16,16,128]{2,1,0:T(8,128)S(1)}, f32[16,16,128]{2,1,0:T(8,128)S(1)}, f32[2,16,128]{2,1,0:T(8,128)S(1)}, f32[18,40,128]{2,1,0:T(8,128)S(1)}, ...) custom-call(f32[18,40,128]{2,1,0:T(8,128)S(1)} %get-tuple-element.48, ...), custom_call_target="tpu_custom_call", output_to_operand_aliasing={{3}: (0, {}), {4}: (1, {}), {5}: (2, {}), {6}: (3, {}), {7}... | custom-call | flops 20000000 | bytes 2000000 | tf_op jit(solution)/shard_map/pallas_call | solution.py:531
  16.3 0.2 collective-permute-done.3.lat
  16.5 0.7 %shard_map.100 = (f32[2,2,16,128]{3,2,1,0:T(8,128)S(1)}, f32[2,40,128]{2,1,0:T(8,128)S(1)}, f32[2,40,128]{2,1,0:T(8,128)S(1)}, f32[2,40,128]{2,1,0:T(8,128)S(1)}...) custom-call(f32[16,16,128]{2,1,0:T(8,128)S(1)} %get-tuple-element.55.adv_t, ...), custom_call_target="tpu_custom_call" | custom-call | flops 2000000 | bytes 2000000 | tf_op jit(solution)/shard_map/pallas_call | solution.py:531
  17.1 1.2 %collective-permute-done.4.fold = f32[56,128]{1,0:T(8,128)S(1)} collective-permute-done((f32[56,128]{1,0:T(8,128)S(1)}, f32[56,128]{1,0:T(8,128)S(1)}, u32[]{:S(2)}, u32[]{:S(2)}) %collective-permute-start.4) | collective-permute-done | bytes 28704 | tf_op jit(solution)/shard_map/ppermute | solution.py:563
  18.3 1.5 %shard_map.101 = (f32[16,16,128]{2,1,0:T(8,128)}, f32[16,16,128]{2,1,0:T(8,128)}) custom-call(f32[16,16,128]{2,1,0:T(8,128)S(1)} %get-tuple-element.55.adv_t, f32[16,16,128]{2,1,0:T(8,128)S(1)} %get-tuple-element.56.adv_s, f32[16,16,128]{2,1,0:T(8,128)S(1)} %get-tuple-element.57.inverse, f32[16,16,128]{2,1,0:T(8,128)S(1)} %get-tuple-element.58.onward, ...), custom_call_target="tpu_custom_call" | custom-call | flops 2000000 | bytes 2000000 | tf_op jit(solution)/shard_map/pallas_call | solution.py:531
  (1 shorter events, 0.0 us)
Async XLA Ops:
  2.4 9.8 %collective-permute-start = (f32[17,16,128]{2,1,0:T(8,128)S(1)}, f32[17,16,128]{2,1,0:T(8,128)S(1)}, u32[]{:S(2)}, u32[]{:S(2)}) collective-permute-start(f32[17,16,128]{2,1,0:T(8,128)S(1)} %get-tuple-element.47), channel_id=1, source_target_pairs={{0,2},{1,3},{2,0},{3,1},{4,6},{5,7},{6,4},{7,5},{8,10},{9,11},{10,... | collective-permute-start | bytes 417800 | tf_op jit(solution)/shard_map/ppermute | solution.py:563
  2.9 11.1 %collective-permute-start.1 = (f32[16,16,128]{2,1,0:T(8,128)S(1)}, f32[16,16,128]{2,1,0:T(8,128)S(1)}, u32[]{:S(2)}, u32[]{:S(2)}) collective-permute-start(f32[16,16,128]{2,1,0:T(8,128)S(1)} %get-tuple-element.54), channel_id=1, source_target_pairs={{0,30},{1,31},{2,4},{3,5},{4,2},{5,3},{6,8},{7,9},{8,6},{9,7},{10,... | collective-permute-start | bytes 393224 | tf_op jit(solution)/shard_map/ppermute | solution.py:563
  8.6 3.7 %collective-permute-start.2 = (f32[16,128]{1,0:T(8,128)S(1)}, f32[16,128]{1,0:T(8,128)S(1)}, u32[]{:S(2)}, u32[]{:S(2)}) collective-permute-start(f32[16,128]{1,0:T(8,128)S(1)} %get-tuple-element.60), channel_id=1, source_target_pairs={{2,4},{3,5},{4,2},{5,3},{6,8},{7,9},{8,6},{9,7},{10,12},{11,13},{1... | collective-permute-start | bytes 24584 | tf_op jit(solution)/shard_map/ppermute | solution.py:563
  12.2 6.1 %collective-permute-start.4 = (f32[56,128]{1,0:T(8,128)S(1)}, f32[56,128]{1,0:T(8,128)S(1)}, u32[]{:S(2)}, u32[]{:S(2)}) collective-permute-start(f32[56,128]{1,0:T(8,128)S(1)} %get-tuple-element.62), channel_id=1, source_target_pairs={{0,30},{1,31},{2,28},{3,29},{4,26},{5,27},{6,24},{7,25},{8,22},{9,... | collective-permute-start | bytes 86024 | tf_op jit(solution)/shard_map/ppermute | solution.py:563
  12.3 4.1 %collective-permute-start.3 = (f32[48,128]{1,0:T(8,128)S(1)}, f32[48,128]{1,0:T(8,128)S(1)}, u32[]{:S(2)}, u32[]{:S(2)}) collective-permute-start(f32[48,128]{1,0:T(8,128)S(1)} %get-tuple-element.61), channel_id=1, source_target_pairs={{0,1},{1,0},{2,3},{3,2},{4,5},{5,4},{6,7},{7,6},{8,9},{9,8},{10,11... | collective-permute-start | bytes 73736 | tf_op jit(solution)/shard_map/ppermute | solution.py:563
